TPU v7x, 128 devices: a whole 4x4x4 slice. The times are simulated.
128 devices in a mesh: gx: 4 (over x_hi, core), gy: 4 (over y), gz: 8 (over x_lo, z).
Axes of the slice: x: 4 (x_hi: 2, x_lo: 2; x = x_hi * 2 + x_lo), y: 4, z: 4, core: 2. Of those that a mesh axis runs over, the one named last changes fastest.
Arguments:
- state: float32 [7, 16, 16, 128, 128], P(None, 'gx', 'gy', 'gz'), may hold values from -6 to 6, as said below
- arms: float32 [3, 16, 16, 128, 128], P(None, 'gx', 'gy', 'gz'), may hold values from -6 to 6
- sphere_frag: int32 [16, 16, 128, 128], P('gx', 'gy', 'gz'), may hold values from 0 to 63
- frag_owner: int32 [8192, 1], P(('gx', 'gy', 'gz')), may hold values from 0 to 127; in each aligned block of 64 rows (0 to 63, 64 to 127, ...) at most 2 rows name the same one
- frag_clump: int32 [8192], P(('gx', 'gy', 'gz')), may hold values from 0 to 47
- tiles: int32 [128, 2048], P(('gx', 'gy', 'gz')), may hold values from 0 to 6911, as said below
- clump_motion: float32 [6, 6144], P(None, ('gx', 'gy', 'gz')), may hold values from -6 to 6
- inv_mass: float32 [6144], P(('gx', 'gy', 'gz')), may hold values from 0.3 to 3
- inv_moment: float32 [6144], P(('gx', 'gy', 'gz')), may hold values from 0.1 to 1
Outputs:
- sphere_next: float32 [6, 16, 16, 128, 128], P(None, 'gx', 'gy', 'gz')
- clump_next: float32 [6, 6144], P(None, ('gx', 'gy', 'gz'))
Inputs may be any that keep to these rules, and one draw needn't show every extreme that they name: `state`: rows 0 to 2 lie in [0, 1), rows 3 to 5 in [-6, 6], row 6 in [0.08, 0.14]. `tiles`: the 2048 codes of one brick are distinct. `frag_owner`: among the 64 fragments of one brick at most 2 name the same owner.
All inputs are finite; a program needn't handle non-finite values.
Results may differ from a plain program's by a relative error of at most 0.0003.
Values sent between devices are 32-bit elements; how exact they have to be, the bound alone decides.
A program may use at most 64 MiB of HBM per device.

v0:
```python
import jax
import jax.numpy as jnp
from jax import lax
from jax.sharding import PartitionSpec as P

CAP = 2


stiffness = 100.0
damping = 2.0
time_step = 0.01
gravity = 9.81
epsilon_sq = 1e-08


def with_halo(x, sides, width):
    for axis, dim in sides:
        devices, length = (lax.axis_size(axis), x.shape[dim])
        up = [(i, (i + 1) % devices) for i in range(devices)]
        down = [(j, i) for i, j in up]
        last = lax.slice_in_dim(x, length - width, length, axis=dim)
        initial = lax.slice_in_dim(x, 0, width, axis=dim)
        before = lax.ppermute(last, axis, up)
        after = lax.ppermute(initial, axis, down)
        x = jnp.concatenate([before, x, after], axis=dim)
    return x


def cross_rows(first, second):
    return jnp.stack(
        [
            first[1] * second[2] - first[2] * second[1],
            first[2] * second[0] - first[0] * second[2],
            first[0] * second[1] - first[1] * second[0],
        ]
    )


def pair_forces(own_block, neighbor_block, cell_shift):
    separation = [
        neighbor_block[axis_k][:, None, :]
        + cell_shift[axis_k][:, None, None]
        - own_block[axis_k][:, :, None]
        for axis_k in range(3)
    ]
    distance = jnp.sqrt(
        separation[0] * separation[0]
        + separation[1] * separation[1]
        + separation[2] * separation[2]
        + epsilon_sq
    )
    radius_own = own_block[6][:, :, None]
    radius_other = neighbor_block[6][:, None, :]
    distinct = (own_block[7][:, :, None] != neighbor_block[7][:, None, :]).astype(jnp.float32)
    intersection = jnp.maximum(radius_own + radius_other - distance, 0.0) * distinct
    reduced = radius_own * radius_other / (radius_own + radius_other)
    closing = (
        sum(
            (
                (neighbor_block[3 + axis_k][:, None, :] - own_block[3 + axis_k][:, :, None])
                * separation[axis_k]
                for axis_k in range(3)
            )
        )
        / distance
    )
    magnitude = (
        stiffness * jnp.sqrt(reduced) * intersection * jnp.sqrt(intersection)
        - damping * jnp.sqrt(reduced * intersection) * closing
    )
    factor = magnitude / distance
    return jnp.stack([-jnp.sum(factor * separation[axis_k], axis=2) for axis_k in range(3)])


def advance(motion, sums, inv_mass, inv_moment):
    pull = jnp.array([0.0, 0.0, gravity], jnp.float32)[:, None]
    velocity = motion[0:3] + time_step * (sums[0:3] * inv_mass[None, :] - pull)
    spin = motion[3:6] + time_step * sums[3:6] * inv_moment[None, :]
    return jnp.concatenate([velocity, spin], axis=0)


def move_spheres(state, arms, motion):
    velocity = motion[0:3]
    spin = motion[3:6]
    half = 0.5 * time_step * spin
    turned = cross_rows(half, arms)
    twice = cross_rows(half, turned)
    scale = 2.0 / (1.0 + half[0] * half[0] + half[1] * half[1] + half[2] * half[2])
    new_arm = arms + scale * (turned + twice)
    position = state[0:3] + time_step * velocity + (new_arm - arms)
    moving = velocity + cross_rows(spin, new_arm)
    return jnp.concatenate([position, moving], axis=0)


def local(
    state, arms, sphere_frag, frag_owner, frag_clump, tiles, clump_motion, inv_mass, inv_moment
):
    cells_x, cells_y, cells_z = (state.shape[1], state.shape[2], state.shape[3])
    slots = state.shape[4]
    cell_count = cells_x * cells_y * cells_z
    owned = inv_mass.shape[0]
    held = frag_clump.shape[0]
    size_x = lax.axis_size("gx")
    size_y = lax.axis_size("gy")
    size_z = lax.axis_size("gz")
    bricks = size_x * size_y * size_z
    owner = frag_owner[:, 0]
    frag_key = (owner * owned + frag_clump).astype(jnp.float32)
    sphere_key = frag_key[sphere_frag]
    full = jnp.concatenate([state, sphere_key[None]], axis=0)
    padded = with_halo(full, (("gx", 1), ("gy", 2), ("gz", 3)), 1)
    span_y = cells_y + 2
    span_z = cells_z + 2
    padded = padded.reshape(8, (cells_x + 2) * span_y * span_z, slots)
    codes = tiles[0]
    block = 64

    def accumulate(total, block_codes):
        own_cell = block_codes // 27
        offset = block_codes % 27
        step_x = offset // 9 - 1
        step_y = offset // 3 % 3 - 1
        step_z = offset % 3 - 1
        cell_x = own_cell // (cells_y * cells_z) + 1
        cell_y = own_cell // cells_z % cells_y + 1
        cell_z = own_cell % cells_z + 1
        own_pad = (cell_x * span_y + cell_y) * span_z + cell_z
        other_pad = ((cell_x + step_x) * span_y + cell_y + step_y) * span_z + cell_z + step_z
        cell_shift = jnp.stack([step_x, step_y, step_z]).astype(jnp.float32)
        forces = pair_forces(
            jnp.take(padded, own_pad, axis=1), jnp.take(padded, other_pad, axis=1), cell_shift
        )
        return (total.at[:, own_cell].add(forces), None)

    force, unused = lax.scan(
        accumulate, jnp.zeros((3, cell_count, slots), jnp.float32), codes.reshape(-1, block)
    )
    lever = arms.reshape(3, cell_count, slots)
    torque = cross_rows(lever, force)
    loads = jnp.concatenate([force, torque], axis=0).reshape(6, -1)
    frag_sums = jax.ops.segment_sum(loads.T, sphere_frag.reshape(-1), num_segments=held).T
    hits = (owner[:, None] == jnp.arange(bricks, dtype=jnp.int32)[None, :]).astype(jnp.int32)
    rank = jnp.sum((jnp.cumsum(hits, axis=0) - hits) * hits, axis=1)
    slot_index = owner * CAP + rank
    payload = jnp.concatenate([frag_sums, (frag_clump + 1).astype(jnp.float32)[None]], axis=0)
    outbox = jnp.zeros((7, bricks * CAP), jnp.float32).at[:, slot_index].set(payload)
    inbox = lax.all_to_all(outbox, ("gx", "gy", "gz"), split_axis=1, concat_axis=1, tiled=True)
    labels = (jnp.arange(owned, dtype=jnp.int32) + 1).astype(jnp.float32)
    which = (inbox[6][:, None] == labels[None, :]).astype(jnp.float32)
    clump_sums = jnp.dot(
        inbox[0:6], which, precision=lax.Precision.HIGHEST, preferred_element_type=jnp.float32
    )
    clump_next = advance(clump_motion, clump_sums, inv_mass, inv_moment)
    column = jnp.clip(inbox[6].astype(jnp.int32) - 1, 0, owned - 1)
    reply = jnp.take(clump_next, column, axis=1)
    answer = lax.all_to_all(reply, ("gx", "gy", "gz"), split_axis=1, concat_axis=1, tiled=True)
    frag_motion = jnp.take(answer, slot_index, axis=1)
    sphere_motion = jnp.take(frag_motion, sphere_frag, axis=1)
    sphere_next = move_spheres(state, arms, sphere_motion)
    return (sphere_next, clump_next)


def solution(mesh):
    return jax.shard_map(
        local,
        mesh=mesh,
        in_specs=(
            P(None, "gx", "gy", "gz", None),
            P(None, "gx", "gy", "gz", None),
            P("gx", "gy", "gz", None),
            P(("gx", "gy", "gz"), None),
            P(("gx", "gy", "gz")),
            P(("gx", "gy", "gz"), None),
            P(None, ("gx", "gy", "gz")),
            P(("gx", "gy", "gz")),
            P(("gx", "gy", "gz")),
        ),
        out_specs=(P(None, "gx", "gy", "gz", None), P(None, ("gx", "gy", "gz"))),
        check_vma=False,
    )
```

profile of v0, /device:TPU:1, one launch (start us, length us, event | category | flops | bytes accessed | tf_op | source)
XLA Modules:
  0.0 1383.9 jit_solution(4066323540185173919)
XLA Ops:
  4.0 193.9 %gather_fusion.2 = f32[32768]{0:T(1024)S(1)} fusion(f32[64]{0:T(128)S(1)} %get-tuple-element.181, s32[32768]{0:T(1024)S(1)} %broadcast_clamp_fusion), kind=kCustom, calls=%fused_computation.2 | custom fusion | bytes 393216 | tf_op jit(solution)/shard_map/gather | solution.py:109
  231.1 765.2 %while.13 = (s32[]{:T(128)}, f32[3,256,128]{2,0,1:T(4,128)S(1)}, s32[32,64]{1,0:T(8,128)S(1)}, f32[8,648,128]{2,0,1:T(8,128)}, s32[]{:T(128)}) while((s32[]{:T(128)}, f32[3,256,128]{2,0,1:T(4,128)S(1)}, s32[32,64]{1,0:T(8,128)S(1)}, f32[8,648,128]{2,0,1:T(8,128)}, s32[]{:T(128)}) %tuple.103), condition=%wide.region_7.9_spmd, body=%wide.region_2.0_spmd.sunk | while | flops 41136192 | bytes 4869185 | solution.py:135
  236.9 15.3 %fusion.66 = (f32[64,128]{1,0:T(8,128)S(1)}, f32[64,128]{1,0:T(8,128)S(1)}, f32[64,128]{1,0:T(8,128)S(1)}) fusion(f32[64,128]{1,0:T(8,128)S(1)} %bitcast.202, f32[64,128]{1,0:T(8,128)S(1)} %broadcast_add_fusion.5, f32[64,128]{1,0:T(8,128)S(1)} %bitcast.197, f32[64,128]{1,0:T(8,128)S(1)} %bitcast.192, f32[64,128]{1,0:T(8,128)S(1)} %bitcast.198, ...), kind=kLoop, calls=%fused_computation.32.clone.1 | loop fusion | flops 40869888 | bytes 622592 | tf_op jit(solution)/shard_map/while/body/eval_jaxpr/reduce_sum | solution.py:72
  260.8 15.3 %fusion.66 = (f32[64,128]{1,0:T(8,128)S(1)}, f32[64,128]{1,0:T(8,128)S(1)}, f32[64,128]{1,0:T(8,128)S(1)}) fusion(f32[64,128]{1,0:T(8,128)S(1)} %bitcast.202, f32[64,128]{1,0:T(8,128)S(1)} %broadcast_add_fusion.5, f32[64,128]{1,0:T(8,128)S(1)} %bitcast.197, f32[64,128]{1,0:T(8,128)S(1)} %bitcast.192, f32[64,128]{1,0:T(8,128)S(1)} %bitcast.198, ...), kind=kLoop, calls=%fused_computation.32.clone.1 | loop fusion | flops 40869888 | bytes 622592 | tf_op jit(solution)/shard_map/while/body/eval_jaxpr/reduce_sum | solution.py:72
  308.6 15.3 %fusion.66 = (f32[64,128]{1,0:T(8,128)S(1)}, f32[64,128]{1,0:T(8,128)S(1)}, f32[64,128]{1,0:T(8,128)S(1)}) fusion(f32[64,128]{1,0:T(8,128)S(1)} %bitcast.202, f32[64,128]{1,0:T(8,128)S(1)} %broadcast_add_fusion.5, f32[64,128]{1,0:T(8,128)S(1)} %bitcast.197, f32[64,128]{1,0:T(8,128)S(1)} %bitcast.192, f32[64,128]{1,0:T(8,128)S(1)} %bitcast.198, ...), kind=kLoop, calls=%fused_computation.32.clone.1 | loop fusion | flops 40869888 | bytes 622592 | tf_op jit(solution)/shard_map/while/body/eval_jaxpr/reduce_sum | solution.py:72
  332.6 15.3 %fusion.66 = (f32[64,128]{1,0:T(8,128)S(1)}, f32[64,128]{1,0:T(8,128)S(1)}, f32[64,128]{1,0:T(8,128)S(1)}) fusion(f32[64,128]{1,0:T(8,128)S(1)} %bitcast.202, f32[64,128]{1,0:T(8,128)S(1)} %broadcast_add_fusion.5, f32[64,128]{1,0:T(8,128)S(1)} %bitcast.197, f32[64,128]{1,0:T(8,128)S(1)} %bitcast.192, f32[64,128]{1,0:T(8,128)S(1)} %bitcast.198, ...), kind=kLoop, calls=%fused_computation.32.clone.1 | loop fusion | flops 40869888 | bytes 622592 | tf_op jit(solution)/shard_map/while/body/eval_jaxpr/reduce_sum | solution.py:72
  380.4 15.3 %fusion.66 = (f32[64,128]{1,0:T(8,128)S(1)}, f32[64,128]{1,0:T(8,128)S(1)}, f32[64,128]{1,0:T(8,128)S(1)}) fusion(f32[64,128]{1,0:T(8,128)S(1)} %bitcast.202, f32[64,128]{1,0:T(8,128)S(1)} %broadcast_add_fusion.5, f32[64,128]{1,0:T(8,128)S(1)} %bitcast.197, f32[64,128]{1,0:T(8,128)S(1)} %bitcast.192, f32[64,128]{1,0:T(8,128)S(1)} %bitcast.198, ...), kind=kLoop, calls=%fused_computation.32.clone.1 | loop fusion | flops 40869888 | bytes 622592 | tf_op jit(solution)/shard_map/while/body/eval_jaxpr/reduce_sum | solution.py:72
  404.3 15.3 %fusion.66 = (f32[64,128]{1,0:T(8,128)S(1)}, f32[64,128]{1,0:T(8,128)S(1)}, f32[64,128]{1,0:T(8,128)S(1)}) fusion(f32[64,128]{1,0:T(8,128)S(1)} %bitcast.202, f32[64,128]{1,0:T(8,128)S(1)} %broadcast_add_fusion.5, f32[64,128]{1,0:T(8,128)S(1)} %bitcast.197, f32[64,128]{1,0:T(8,128)S(1)} %bitcast.192, f32[64,128]{1,0:T(8,128)S(1)} %bitcast.198, ...), kind=kLoop, calls=%fused_computation.32.clone.1 | loop fusion | flops 40869888 | bytes 622592 | tf_op jit(solution)/shard_map/while/body/eval_jaxpr/reduce_sum | solution.py:72
  428.2 15.3 %fusion.66 = (f32[64,128]{1,0:T(8,128)S(1)}, f32[64,128]{1,0:T(8,128)S(1)}, f32[64,128]{1,0:T(8,128)S(1)}) fusion(f32[64,128]{1,0:T(8,128)S(1)} %bitcast.202, f32[64,128]{1,0:T(8,128)S(1)} %broadcast_add_fusion.5, f32[64,128]{1,0:T(8,128)S(1)} %bitcast.197, f32[64,128]{1,0:T(8,128)S(1)} %bitcast.192, f32[64,128]{1,0:T(8,128)S(1)} %bitcast.198, ...), kind=kLoop, calls=%fused_computation.32.clone.1 | loop fusion | flops 40869888 | bytes 622592 | tf_op jit(solution)/shard_map/while/body/eval_jaxpr/reduce_sum | solution.py:72
  476.0 15.3 %fusion.66 = (f32[64,128]{1,0:T(8,128)S(1)}, f32[64,128]{1,0:T(8,128)S(1)}, f32[64,128]{1,0:T(8,128)S(1)}) fusion(f32[64,128]{1,0:T(8,128)S(1)} %bitcast.202, f32[64,128]{1,0:T(8,128)S(1)} %broadcast_add_fusion.5, f32[64,128]{1,0:T(8,128)S(1)} %bitcast.197, f32[64,128]{1,0:T(8,128)S(1)} %bitcast.192, f32[64,128]{1,0:T(8,128)S(1)} %bitcast.198, ...), kind=kLoop, calls=%fused_computation.32.clone.1 | loop fusion | flops 40869888 | bytes 622592 | tf_op jit(solution)/shard_map/while/body/eval_jaxpr/reduce_sum | solution.py:72
  499.9 15.3 %fusion.66 = (f32[64,128]{1,0:T(8,128)S(1)}, f32[64,128]{1,0:T(8,128)S(1)}, f32[64,128]{1,0:T(8,128)S(1)}) fusion(f32[64,128]{1,0:T(8,128)S(1)} %bitcast.202, f32[64,128]{1,0:T(8,128)S(1)} %broadcast_add_fusion.5, f32[64,128]{1,0:T(8,128)S(1)} %bitcast.197, f32[64,128]{1,0:T(8,128)S(1)} %bitcast.192, f32[64,128]{1,0:T(8,128)S(1)} %bitcast.198, ...), kind=kLoop, calls=%fused_computation.32.clone.1 | loop fusion | flops 40869888 | bytes 622592 | tf_op jit(solution)/shard_map/while/body/eval_jaxpr/reduce_sum | solution.py:72
  547.8 15.3 %fusion.66 = (f32[64,128]{1,0:T(8,128)S(1)}, f32[64,128]{1,0:T(8,128)S(1)}, f32[64,128]{1,0:T(8,128)S(1)}) fusion(f32[64,128]{1,0:T(8,128)S(1)} %bitcast.202, f32[64,128]{1,0:T(8,128)S(1)} %broadcast_add_fusion.5, f32[64,128]{1,0:T(8,128)S(1)} %bitcast.197, f32[64,128]{1,0:T(8,128)S(1)} %bitcast.192, f32[64,128]{1,0:T(8,128)S(1)} %bitcast.198, ...), kind=kLoop, calls=%fused_computation.32.clone.1 | loop fusion | flops 40869888 | bytes 622592 | tf_op jit(solution)/shard_map/while/body/eval_jaxpr/reduce_sum | solution.py:72
  571.7 15.3 %fusion.66 = (f32[64,128]{1,0:T(8,128)S(1)}, f32[64,128]{1,0:T(8,128)S(1)}, f32[64,128]{1,0:T(8,128)S(1)}) fusion(f32[64,128]{1,0:T(8,128)S(1)} %bitcast.202, f32[64,128]{1,0:T(8,128)S(1)} %broadcast_add_fusion.5, f32[64,128]{1,0:T(8,128)S(1)} %bitcast.197, f32[64,128]{1,0:T(8,128)S(1)} %bitcast.192, f32[64,128]{1,0:T(8,128)S(1)} %bitcast.198, ...), kind=kLoop, calls=%fused_computation.32.clone.1 | loop fusion | flops 40869888 | bytes 622592 | tf_op jit(solution)/shard_map/while/body/eval_jaxpr/reduce_sum | solution.py:72
  595.6 15.3 %fusion.66 = (f32[64,128]{1,0:T(8,128)S(1)}, f32[64,128]{1,0:T(8,128)S(1)}, f32[64,128]{1,0:T(8,128)S(1)}) fusion(f32[64,128]{1,0:T(8,128)S(1)} %bitcast.202, f32[64,128]{1,0:T(8,128)S(1)} %broadcast_add_fusion.5, f32[64,128]{1,0:T(8,128)S(1)} %bitcast.197, f32[64,128]{1,0:T(8,128)S(1)} %bitcast.192, f32[64,128]{1,0:T(8,128)S(1)} %bitcast.198, ...), kind=kLoop, calls=%fused_computation.32.clone.1 | loop fusion | flops 40869888 | bytes 622592 | tf_op jit(solution)/shard_map/while/body/eval_jaxpr/reduce_sum | solution.py:72
  643.4 15.3 %fusion.66 = (f32[64,128]{1,0:T(8,128)S(1)}, f32[64,128]{1,0:T(8,128)S(1)}, f32[64,128]{1,0:T(8,128)S(1)}) fusion(f32[64,128]{1,0:T(8,128)S(1)} %bitcast.202, f32[64,128]{1,0:T(8,128)S(1)} %broadcast_add_fusion.5, f32[64,128]{1,0:T(8,128)S(1)} %bitcast.197, f32[64,128]{1,0:T(8,128)S(1)} %bitcast.192, f32[64,128]{1,0:T(8,128)S(1)} %bitcast.198, ...), kind=kLoop, calls=%fused_computation.32.clone.1 | loop fusion | flops 40869888 | bytes 622592 | tf_op jit(solution)/shard_map/while/body/eval_jaxpr/reduce_sum | solution.py:72
  715.2 15.3 %fusion.66 = (f32[64,128]{1,0:T(8,128)S(1)}, f32[64,128]{1,0:T(8,128)S(1)}, f32[64,128]{1,0:T(8,128)S(1)}) fusion(f32[64,128]{1,0:T(8,128)S(1)} %bitcast.202, f32[64,128]{1,0:T(8,128)S(1)} %broadcast_add_fusion.5, f32[64,128]{1,0:T(8,128)S(1)} %bitcast.197, f32[64,128]{1,0:T(8,128)S(1)} %bitcast.192, f32[64,128]{1,0:T(8,128)S(1)} %bitcast.198, ...), kind=kLoop, calls=%fused_computation.32.clone.1 | loop fusion | flops 40869888 | bytes 622592 | tf_op jit(solution)/shard_map/while/body/eval_jaxpr/reduce_sum | solution.py:72
  739.1 15.3 %fusion.66 = (f32[64,128]{1,0:T(8,128)S(1)}, f32[64,128]{1,0:T(8,128)S(1)}, f32[64,128]{1,0:T(8,128)S(1)}) fusion(f32[64,128]{1,0:T(8,128)S(1)} %bitcast.202, f32[64,128]{1,0:T(8,128)S(1)} %broadcast_add_fusion.5, f32[64,128]{1,0:T(8,128)S(1)} %bitcast.197, f32[64,128]{1,0:T(8,128)S(1)} %bitcast.192, f32[64,128]{1,0:T(8,128)S(1)} %bitcast.198, ...), kind=kLoop, calls=%fused_computation.32.clone.1 | loop fusion | flops 40869888 | bytes 622592 | tf_op jit(solution)/shard_map/while/body/eval_jaxpr/reduce_sum | solution.py:72
  763.0 15.3 %fusion.66 = (f32[64,128]{1,0:T(8,128)S(1)}, f32[64,128]{1,0:T(8,128)S(1)}, f32[64,128]{1,0:T(8,128)S(1)}) fusion(f32[64,128]{1,0:T(8,128)S(1)} %bitcast.202, f32[64,128]{1,0:T(8,128)S(1)} %broadcast_add_fusion.5, f32[64,128]{1,0:T(8,128)S(1)} %bitcast.197, f32[64,128]{1,0:T(8,128)S(1)} %bitcast.192, f32[64,128]{1,0:T(8,128)S(1)} %bitcast.198, ...), kind=kLoop, calls=%fused_computation.32.clone.1 | loop fusion | flops 40869888 | bytes 622592 | tf_op jit(solution)/shard_map/while/body/eval_jaxpr/reduce_sum | solution.py:72
  786.9 15.3 %fusion.66 = (f32[64,128]{1,0:T(8,128)S(1)}, f32[64,128]{1,0:T(8,128)S(1)}, f32[64,128]{1,0:T(8,128)S(1)}) fusion(f32[64,128]{1,0:T(8,128)S(1)} %bitcast.202, f32[64,128]{1,0:T(8,128)S(1)} %broadcast_add_fusion.5, f32[64,128]{1,0:T(8,128)S(1)} %bitcast.197, f32[64,128]{1,0:T(8,128)S(1)} %bitcast.192, f32[64,128]{1,0:T(8,128)S(1)} %bitcast.198, ...), kind=kLoop, calls=%fused_computation.32.clone.1 | loop fusion | flops 40869888 | bytes 622592 | tf_op jit(solution)/shard_map/while/body/eval_jaxpr/reduce_sum | solution.py:72
  858.6 15.3 %fusion.66 = (f32[64,128]{1,0:T(8,128)S(1)}, f32[64,128]{1,0:T(8,128)S(1)}, f32[64,128]{1,0:T(8,128)S(1)}) fusion(f32[64,128]{1,0:T(8,128)S(1)} %bitcast.202, f32[64,128]{1,0:T(8,128)S(1)} %broadcast_add_fusion.5, f32[64,128]{1,0:T(8,128)S(1)} %bitcast.197, f32[64,128]{1,0:T(8,128)S(1)} %bitcast.192, f32[64,128]{1,0:T(8,128)S(1)} %bitcast.198, ...), kind=kLoop, calls=%fused_computation.32.clone.1 | loop fusion | flops 40869888 | bytes 622592 | tf_op jit(solution)/shard_map/while/body/eval_jaxpr/reduce_sum | solution.py:72
  882.6 15.3 %fusion.66 = (f32[64,128]{1,0:T(8,128)S(1)}, f32[64,128]{1,0:T(8,128)S(1)}, f32[64,128]{1,0:T(8,128)S(1)}) fusion(f32[64,128]{1,0:T(8,128)S(1)} %bitcast.202, f32[64,128]{1,0:T(8,128)S(1)} %broadcast_add_fusion.5, f32[64,128]{1,0:T(8,128)S(1)} %bitcast.197, f32[64,128]{1,0:T(8,128)S(1)} %bitcast.192, f32[64,128]{1,0:T(8,128)S(1)} %bitcast.198, ...), kind=kLoop, calls=%fused_computation.32.clone.1 | loop fusion | flops 40869888 | bytes 622592 | tf_op jit(solution)/shard_map/while/body/eval_jaxpr/reduce_sum | solution.py:72
  930.4 15.3 %fusion.66 = (f32[64,128]{1,0:T(8,128)S(1)}, f32[64,128]{1,0:T(8,128)S(1)}, f32[64,128]{1,0:T(8,128)S(1)}) fusion(f32[64,128]{1,0:T(8,128)S(1)} %bitcast.202, f32[64,128]{1,0:T(8,128)S(1)} %broadcast_add_fusion.5, f32[64,128]{1,0:T(8,128)S(1)} %bitcast.197, f32[64,128]{1,0:T(8,128)S(1)} %bitcast.192, f32[64,128]{1,0:T(8,128)S(1)} %bitcast.198, ...), kind=kLoop, calls=%fused_computation.32.clone.1 | loop fusion | flops 40869888 | bytes 622592 | tf_op jit(solution)/shard_map/while/body/eval_jaxpr/reduce_sum | solution.py:72
  1006.1 216.9 %scatter_custom_fusion.1 = f32[64,6]{1,0:T(8,128)S(1)} fusion(s32[32768]{0:T(1024)S(1)} %bitcast.204, f32[32768,6]{1,0:T(8,128)} %copy.87, f32[]{:T(128)} %constant.269.clone.1), kind=kCustom, calls=%fused_computation.151 | custom fusion | flops 196608 | bytes 2048 | tf_op jit(solution)/shard_map/scatter-add | solution.py:141
  1262.2 109.0 %gather_fusion.5 = f32[32768,6]{1,0:T(8,128)} fusion(f32[6,64]{0,1:T(8,128)S(1)} %select_bitcast_fusion.3, s32[32768]{0:T(1024)S(1)} %broadcast_clamp_fusion), kind=kCustom, calls=%fused_computation.5 | custom fusion | bytes 1703936 | tf_op jit(solution)/shard_map/jit(_take)/gather | solution.py:158
  (871 shorter events, 552.5 us)
Async XLA Ops:
  4.0 198.2 %copy-start.3 = (s32[64,1]{0,1:T(1,128)S(1)}, s32[64,1]{0,1:T(1,128)}, u32[]{:S(2)}) copy-start(s32[64,1]{0,1:T(1,128)} %param.17) | copy-start | bytes 772
  4.0 199.1 %copy-start.4 = (s32[1,2048]{1,0:T(1,128)S(1)}, s32[1,2048]{1,0:T(1,128)}, u32[]{:S(2)}) copy-start(s32[1,2048]{1,0:T(1,128)} %param.19) | copy-start | bytes 24580
  4.0 199.9 %copy-start.1 = (s32[4,4,16,128]{3,2,1,0:T(8,128)S(1)}, s32[4,4,16,128]{3,2,1,0:T(8,128)}, u32[]{:S(2)}) copy-start(s32[4,4,16,128]{3,2,1,0:T(8,128)} %param.16) | copy-start | bytes 393220
  197.9 14.7 %copy-start = (f32[3,4,4,16,128]{4,3,2,1,0:T(8,128)S(1)}, f32[3,4,4,16,128]{4,3,2,1,0:T(8,128)}, u32[]{:S(2)}) copy-start(f32[3,4,4,16,128]{4,3,2,1,0:T(8,128)} %param.15) | copy-start | bytes 1179652
  197.9 27.9 %copy-start.8 = (f32[48]{0:T(128)S(1)}, f32[48]{0:T(128)}, u32[]{:S(2)}) copy-start(f32[48]{0:T(128)} %param.22) | copy-start | bytes 580
  198.0 9.6 collective-permute-start
  202.2 7.3 collective-permute-start.1
  209.6 11.8 collective-permute-start.2
  211.0 11.0 collective-permute-start.3
  222.1 7.2 collective-permute-start.4
  223.8 5.5 collective-permute-start.5
  997.0 248.4 %copy-start.5 = (f32[6,48]{1,0:T(8,128)S(1)}, f32[6,48]{1,0:T(8,128)}, u32[]{:S(2)}) copy-start(f32[6,48]{1,0:T(8,128)} %param.20) | copy-start | bytes 3460
  997.0 248.4 %copy-start.6 = (f32[48]{0:T(128)S(1)}, f32[48]{0:T(128)}, u32[]{:S(2)}) copy-start(f32[48]{0:T(128)} %param.21) | copy-start | bytes 580
  997.0 248.4 %copy-start.7 = (f32[3]{0:T(128)S(1)}, f32[3]{0:T(128)}, u32[]{:S(2)}) copy-start(f32[3]{0:T(128)} %constant.286) | copy-start | bytes 40
  1224.5 19.7 %all-to-all-start = ((f32[7,128,2]{0,2,1:T(2,128)}), f32[7,128,2]{0,2,1:T(2,128)S(1)}, u32[]{:S(2)}, u32[]{:S(2)}) async-start(f32[7,128,2]{0,2,1:T(2,128)} %bitcast.50), calls=%async_computation | async-start | bytes 262144 | tf_op jit(solution)/shard_map/all_to_all | solution.py:147
  1245.5 135.7 %copy-start.2 = (f32[6,48]{1,0:T(8,128)}, f32[6,48]{1,0:T(8,128)S(1)}, u32[]{:S(2)}) copy-start(f32[6,48]{1,0:T(8,128)S(1)} %pad_maximum_fusion.14) | copy-start | bytes 3460
  1247.4 14.1 %all-to-all-start.1 = ((f32[6,128,2]{0,2,1:T(2,128)}), f32[6,128,2]{0,2,1:T(2,128)S(1)}, u32[]{:S(2)}, u32[]{:S(2)}) async-start(f32[6,128,2]{0,2,1:T(2,128)} %broadcast_select_fusion), calls=%async_computation.1 | async-start | bytes 262144 | tf_op jit(solution)/shard_map/all_to_all | solution.py:156
where the time goes:
time: 1390 us; the launch traced here: 1380 us
  other arithmetic  822 us (59%)
  local copies, waits for them, and re-layouts  492 us (35%)
  waiting for transfers between devices  38.5 us (3%)
  starting transfers between devices  24.6 us (2%)
    reduce_sum x32, other arithmetic, pair_forces(): jnp.sum(factor * separation[axis_k], axis=2)  488 us
    scatter-add x1, other arithmetic, local(): jax.ops.segment_sum(loads.T, sphere_frag.reshape(-1), num_segments=held)  217 us
    gather x1, local copies, waits for them, and re-layouts, local(): sphere_key = frag_key[sphere_frag]  194 us
    gather x2, local copies, waits for them, and re-layouts, local(): sphere_motion = jnp.take(frag_motion, sphere_frag, axis=1)  119 us
    scatter-add x32, other arithmetic, accumulate(): return (total.at[:, own_cell].add(forces), None)  87.6 us
    gather x32, local copies, waits for them, and re-layouts, accumulate(): jnp.take(padded, own_pad, axis=1)  75 us
    gather x32, local copies, waits for them, and re-layouts, accumulate(): jnp.take(padded, other_pad, axis=1)  75 us
  transfers between devices with their start and end apart: 8, of which 7 were waited for; matrix products, arithmetic and copies ran while one was open for 0% of the time, Pallas kernels for 0%

commit v1 on v0

v1 whole, which is shorter than its diff:
```python
import functools

import jax
import jax.numpy as jnp
from jax import lax
from jax.experimental import pallas as pl
from jax.experimental.pallas import tpu as pltpu
from jax.sharding import PartitionSpec as P

CAP = 2
REACH = 0.14001
time_step = 0.01
gravity = 9.81
epsilon_sq = 1e-08
UNROLL = 8
VMEM = pl.BlockSpec(memory_space=pltpu.VMEM)
SMEM = pl.BlockSpec(memory_space=pltpu.SMEM)


def lane_take(rows, index):
    return jnp.take_along_axis(rows, index, axis=1, mode="promise_in_bounds")


def cross_rows(first, second):
    return [
        first[1] * second[2] - first[2] * second[1],
        first[2] * second[0] - first[0] * second[2],
        first[0] * second[1] - first[1] * second[0],
    ]


def pack_kernel(state, frag, table, out):
    keys = jnp.broadcast_to(table[...], (8, 128))
    for g in range(frag.shape[0] // 8):
        rows = pl.ds(8 * g, 8)
        for k in range(7):
            out[pl.ds(64 * g + k, 8, stride=8), :] = state[k, rows, :]
        out[pl.ds(64 * g + 7, 8, stride=8), :] = lane_take(keys, frag[rows, :])


def tile_parts(code, ny, nz):
    own = (code * 38837) >> 20
    offset = code - 27 * own
    step_x = ((offset * 57) >> 9) - 1
    left = offset - 9 * (step_x + 1)
    step_y = ((left * 11) >> 5) - 1
    step_z = left - 3 * (step_y + 1) - 1
    cell = ((own >> 6) + 1 + step_x) * (ny * nz) + (((own >> 4) & 3) + 1 + step_y) * nz + (own & 15) + 1 + step_z
    return own, offset, cell


def tiles_kernel(
    codes, cells, arms, frag, out, cand, mask, perm, counts, counts_s, lens, lists, shifts, cols, loads, sem
):
    tiles = codes.shape[0]
    pad = cells.shape[0] // 8
    ny, nz = 6, 18
    chunks = lists.shape[1]
    sub = lax.broadcasted_iota(jnp.int32, (8, 128), 0)
    lane = lax.broadcasted_iota(jnp.int32, (8, 128), 1)

    @pl.loop(0, pad // 8)
    def _(g):
        base = pl.multiple_of(g * 64, 64)
        pos = [cells[pl.ds(base + k, 8, stride=8), :] for k in range(3)]
        reach = cells[pl.ds(base + 6, 8, stride=8), :] + REACH
        reach = reach * reach
        near = [p * p for p in pos]
        far = [(1.0 - p) * (1.0 - p) for p in pos]
        bits = jnp.full((8, 128), 1 << 13, jnp.int32)
        for o in range(27):
            steps = (o // 9 - 1, o // 3 % 3 - 1, o % 3 - 1)
            terms = [near[k] if s > 0 else far[k] for k, s in enumerate(steps) if s]
            if not terms:
                continue
            bits = bits | jnp.where(sum(terms[1:], terms[0]) <= reach, 1 << o, 0)
        cand[pl.ds(pl.multiple_of(g * 8, 8), 8), :] = bits

    @pl.loop(0, 27)
    def _(o):
        step_x = ((o * 57) >> 9) - 1
        left = o - 9 * (step_x + 1)
        step_y = ((left * 11) >> 5) - 1
        step_z = left - 3 * (step_y + 1) - 1
        value = jnp.where(sub == 0, step_x, jnp.where(sub == 1, step_y, jnp.where(sub == 2, step_z, 0)))
        shifts[o] = value.astype(jnp.float32)

    @pl.loop(0, 256)
    def _(c):
        lens[c] = 0

    @pl.loop(0, tiles // 16)
    def _(b):
        for u in range(16):
            t = b * 16 + u
            own, offset, cell = tile_parts(codes[t], ny, nz)
            mask[pl.ds(t, 1), :] = (cand[pl.ds(cell, 1), :] >> offset) & 1

    row = lax.broadcasted_iota(jnp.int32, (128, 128), 0)
    col = lax.broadcasted_iota(jnp.int32, (128, 128), 1)
    before = (row < col).astype(jnp.bfloat16)
    ones = jnp.ones((8, 128), jnp.bfloat16)

    @pl.loop(0, tiles // 128)
    def _(b):
        rows = pl.ds(pl.multiple_of(b * 128, 128), 128)
        active = mask[rows, :]
        flags = active.astype(jnp.float32).astype(jnp.bfloat16)
        rank = jnp.dot(flags, before, preferred_element_type=jnp.float32).astype(jnp.int32)
        number = lax.dot_general(ones, flags, (((1,), (1,)), ((), ())), preferred_element_type=jnp.float32)
        counts[pl.ds(b, 1), :] = number[0:1].astype(jnp.int32)
        value = jnp.where(active > 0, ((col - rank) << 7) | col, 0)
        for bit in range(7):
            moved = pltpu.roll(value, 128 - (1 << bit), axis=1)
            flag = 1 << (7 + bit)
            value = jnp.where((moved & flag) != 0, moved, jnp.where((value & flag) != 0, 0, value))
        perm[rows, :] = value & 127

    copy = pltpu.make_async_copy(counts, counts_s, sem)
    copy.start()
    copy.wait()

    def append(own, sorted_rows, number):
        at = lens[own]
        lens[own] = at + number
        chunk = at >> 7
        turn = at & 127
        turned = pltpu.roll(sorted_rows, turn, axis=1)
        lists[own, chunk] = jnp.where(lane >= turn, turned, lists[own, chunk])
        lists[own, chunk + 1] = turned

    @pl.loop(0, tiles // 8)
    def _(b):
        for u in range(8):
            t = b * 8 + u
            own, offset, cell = tile_parts(codes[t], ny, nz)
            values = cells[pl.ds(pl.multiple_of(cell * 8, 8), 8), :]
            index = jnp.broadcast_to(perm[pl.ds(t, 1), :], (8, 128))
            append(own, lane_take(values, index) + shifts[offset], counts_s[t >> 7, t & 127])

    dummy = jnp.where(sub < 3, 1000.0, 0.1)

    @pl.loop(0, 32)
    def _(b):
        for u in range(8):
            append(b * 8 + u, dummy, 0)

    @pl.loop(0, 16)
    def _(g):
        most = lax.fori_loop(0, 16, lambda k, m: jnp.maximum(m, lens[g * 16 + k]), 0)

        @pl.loop(0, (most + 127) // 128)
        def _(m):
            block = lists[pl.ds(g * 16, 16), m].reshape(128, 128)
            cols[pl.ds(pl.multiple_of(m * 128, 128), 128), :] = block.T

        first = ((g >> 2) + 1) * (ny * nz) + ((g & 3) + 1) * nz + 1

        @pl.loop(0, 16)
        def _(cc):
            cell = g * 16 + cc
            mine = cells[pl.ds(pl.multiple_of((first + cc) * 8, 8), 8), :]
            own = [jnp.broadcast_to(mine[k : k + 1], (8, 128)) for k in range(8)]
            turn = (128 - 8 * cc) & 127

            def step(it, total):
                for u in range(UNROLL):
                    at = pl.multiple_of(it * (8 * UNROLL) + 8 * u, 8)
                    data = pltpu.roll(cols[pl.ds(at, 8), :], turn, axis=1)
                    other = [jnp.broadcast_to(data[:, k : k + 1], (8, 128)) for k in range(8)]
                    apart = [other[k] - own[k] for k in range(3)]
                    square = apart[0] * apart[0] + apart[1] * apart[1] + apart[2] * apart[2] + epsilon_sq
                    inverse = lax.rsqrt(square)
                    reach = own[6] + other[6]
                    depth = jnp.where(own[7] != other[7], jnp.maximum(reach - square * inverse, 0.0), 0.0)
                    closing = (
                        (other[3] - own[3]) * apart[0]
                        + (other[4] - own[4]) * apart[1]
                        + (other[5] - own[5]) * apart[2]
                    )
                    along = closing * inverse - 50.0 * depth
                    area = own[6] * other[6] * depth
                    factor = area * lax.rsqrt(jnp.maximum(area * reach, 1e-20)) * along * inverse
                    total = tuple(total[k] + factor * apart[k] for k in range(3))
                return total

            zero = jnp.zeros((8, 128), jnp.float32)
            count = (lens[cell] + (8 * UNROLL - 1)) // (8 * UNROLL)
            total = lax.fori_loop(0, count, step, (zero, zero, zero))
            force = [2.0 * jnp.sum(t, axis=0, keepdims=True) for t in total]
            lever = [arms[k, pl.ds(cell, 1), :] for k in range(3)]
            turn_rows = cross_rows(lever, force)
            at = pl.multiple_of(cell * 128, 128)
            for k in range(3):
                loads[pl.ds(k, 1), pl.ds(at, 128)] = force[k]
                loads[pl.ds(3 + k, 1), pl.ds(at, 128)] = turn_rows[k]
            loads[pl.ds(6, 1), pl.ds(at, 128)] = frag[pl.ds(cell, 1), :].astype(jnp.float32)
            loads[pl.ds(7, 1), pl.ds(at, 128)] = jnp.zeros((1, 128), jnp.float32)

    span = 1024
    ids = lax.broadcasted_iota(jnp.int32, (128, span), 0).astype(jnp.float32)

    def gather(b, total):
        at = pl.ds(pl.multiple_of(b * span, span), span)
        which = (ids == loads[6:7, at]).astype(jnp.float32)
        return total + lax.dot_general(
            loads[:, at], which, (((1,), (1,)), ((), ())), precision=lax.Precision.HIGHEST,
            preferred_element_type=jnp.float32,
        )

    out[...] = lax.fori_loop(0, loads.shape[1] // span, gather, jnp.zeros((8, 128), jnp.float32))


def move_kernel(state, arms, frag, table, out):
    rows_of = [jnp.broadcast_to(table[k : k + 1, :], (8, 128)) for k in range(6)]
    for g in range(frag.shape[0] // 8):
        rows = pl.ds(8 * g, 8)
        index = frag[rows, :]
        motion = [lane_take(r, index) for r in rows_of]
        velocity, spin = motion[0:3], motion[3:6]
        lever = [arms[k, rows, :] for k in range(3)]
        half = [0.5 * time_step * w for w in spin]
        turned = cross_rows(half, lever)
        twice = cross_rows(half, turned)
        scale = 2.0 / (1.0 + half[0] * half[0] + half[1] * half[1] + half[2] * half[2])
        moved = [lever[k] + scale * (turned[k] + twice[k]) for k in range(3)]
        swing = cross_rows(spin, moved)
        for k in range(3):
            out[k, rows, :] = state[k, rows, :] + time_step * velocity[k] + (moved[k] - lever[k])
            out[3 + k, rows, :] = velocity[k] + swing[k]


def pack(state, frag, table):
    n = frag.shape[0]
    part = n // 4
    return pl.pallas_call(
        pack_kernel,
        grid=(4,),
        in_specs=[
            pl.BlockSpec((7, part, 128), lambda i: (0, i, 0)),
            pl.BlockSpec((part, 128), lambda i: (i, 0)),
            pl.BlockSpec((1, 128), lambda i: (0, 0)),
        ],
        out_specs=pl.BlockSpec((8 * part, 128), lambda i: (i, 0)),
        out_shape=jax.ShapeDtypeStruct((8 * n, 128), jnp.float32),
        name="pack",
    )(state, frag, table)


def forces(codes, cells, arms, frag):
    tiles = codes.shape[0]
    return pl.pallas_call(
        tiles_kernel,
        in_specs=[SMEM, VMEM, VMEM, VMEM],
        out_specs=VMEM,
        out_shape=jax.ShapeDtypeStruct((8, 128), jnp.float32),
        scratch_shapes=[
            pltpu.VMEM((cells.shape[0] // 8, 128), jnp.int32),
            pltpu.VMEM((tiles, 128), jnp.int32),
            pltpu.VMEM((tiles, 128), jnp.int32),
            pltpu.VMEM((tiles // 128, 128), jnp.int32),
            pltpu.SMEM((tiles // 128, 128), jnp.int32),
            pltpu.SMEM((256,), jnp.int32),
            pltpu.VMEM((256, 29, 8, 128), jnp.float32),
            pltpu.VMEM((27, 8, 128), jnp.float32),
            pltpu.VMEM((29 * 128, 128), jnp.float32),
            pltpu.VMEM((8, 256 * 128), jnp.float32),
            pltpu.SemaphoreType.DMA,
        ],
        compiler_params=pltpu.CompilerParams(vmem_limit_bytes=60 * 1024 * 1024),
        name="forces",
    )(codes, cells, arms, frag)


def move(state, arms, frag, table):
    n = frag.shape[0]
    part = n // 4
    return pl.pallas_call(
        move_kernel,
        grid=(4,),
        in_specs=[
            pl.BlockSpec((3, part, 128), lambda i: (0, i, 0)),
            pl.BlockSpec((3, part, 128), lambda i: (0, i, 0)),
            pl.BlockSpec((part, 128), lambda i: (i, 0)),
            pl.BlockSpec((8, 128), lambda i: (0, 0)),
        ],
        out_specs=pl.BlockSpec((6, part, 128), lambda i: (0, i, 0)),
        out_shape=jax.ShapeDtypeStruct((6, n, 128), jnp.float32),
        name="move",
    )(state, arms, frag, table)


def with_halo(x, sides):
    for axis, dim in sides:
        devices, length = (lax.axis_size(axis), x.shape[dim])
        up = [(i, (i + 1) % devices) for i in range(devices)]
        down = [(j, i) for i, j in up]
        last = lax.slice_in_dim(x, length - 1, length, axis=dim)
        initial = lax.slice_in_dim(x, 0, 1, axis=dim)
        before = lax.ppermute(last, axis, up)
        after = lax.ppermute(initial, axis, down)
        x = jnp.concatenate([before, x, after], axis=dim)
    return x


def advance(motion, sums, inv_mass, inv_moment):
    pull = jnp.array([0.0, 0.0, gravity], jnp.float32)[:, None]
    velocity = motion[0:3] + time_step * (sums[0:3] * inv_mass[None, :] - pull)
    spin = motion[3:6] + time_step * sums[3:6] * inv_moment[None, :]
    return jnp.concatenate([velocity, spin], axis=0)


def local(state, arms, sphere_frag, frag_owner, frag_clump, tiles, clump_motion, inv_mass, inv_moment):
    cx, cy, cz, slots = state.shape[1:]
    count = cx * cy * cz
    owned = inv_mass.shape[0]
    held = frag_clump.shape[0]
    bricks = lax.axis_size("gx") * lax.axis_size("gy") * lax.axis_size("gz")
    owner = frag_owner[:, 0]
    frag = sphere_frag.reshape(count, slots)
    key = (owner * owned + frag_clump).astype(jnp.float32)
    own_cells = pack(state.reshape(7, count, slots), frag, jnp.pad(key, (0, 128 - held))[None])
    padded = with_halo(own_cells.reshape(cx, cy, cz, 8, slots), (("gx", 0), ("gy", 1), ("gz", 2)))
    frag_sums = forces(tiles[0], padded.reshape(-1, slots), arms.reshape(3, count, slots), frag)[0:6, 0:held]

    hits = (owner[:, None] == jnp.arange(bricks, dtype=jnp.int32)[None, :]).astype(jnp.int32)
    rank = jnp.sum((jnp.cumsum(hits, axis=0) - hits) * hits, axis=1)
    slot_index = owner * CAP + rank
    payload = jnp.concatenate([frag_sums, (frag_clump + 1).astype(jnp.float32)[None]], axis=0)
    outbox = jnp.zeros((7, bricks * CAP), jnp.float32).at[:, slot_index].set(payload)
    inbox = lax.all_to_all(outbox, ("gx", "gy", "gz"), split_axis=1, concat_axis=1, tiled=True)
    labels = (jnp.arange(owned, dtype=jnp.int32) + 1).astype(jnp.float32)
    which = (inbox[6][:, None] == labels[None, :]).astype(jnp.float32)
    clump_sums = jnp.dot(
        inbox[0:6], which, precision=lax.Precision.HIGHEST, preferred_element_type=jnp.float32
    )
    clump_next = advance(clump_motion, clump_sums, inv_mass, inv_moment)
    column = jnp.clip(inbox[6].astype(jnp.int32) - 1, 0, owned - 1)
    reply = jnp.take(clump_next, column, axis=1)
    answer = lax.all_to_all(reply, ("gx", "gy", "gz"), split_axis=1, concat_axis=1, tiled=True)
    frag_motion = jnp.take(answer, slot_index, axis=1)
    table = jnp.pad(frag_motion, ((0, 2), (0, 128 - held)))
    sphere_next = move(state.reshape(7, count, slots), arms.reshape(3, count, slots), frag, table)
    return sphere_next.reshape(6, cx, cy, cz, slots), clump_next


def solution(mesh):
    return jax.shard_map(
        local,
        mesh=mesh,
        in_specs=(
            P(None, "gx", "gy", "gz", None),
            P(None, "gx", "gy", "gz", None),
            P("gx", "gy", "gz", None),
            P(("gx", "gy", "gz"), None),
            P(("gx", "gy", "gz")),
            P(("gx", "gy", "gz"), None),
            P(None, ("gx", "gy", "gz")),
            P(("gx", "gy", "gz")),
            P(("gx", "gy", "gz")),
        ),
        out_specs=(P(None, "gx", "gy", "gz", None), P(None, ("gx", "gy", "gz"))),
        check_vma=False,
    )
```

time: 1390 us -> 364 us (0.26)
  other arithmetic: 822 us -> 5.55 us
  local copies, waits for them, and re-layouts: 492 us -> 6.21 us
  Pallas kernels: 0 us -> 275 us
    reduce_sum x32 -> x0, other arithmetic: 488 us -> none  [pair_forces(): jnp.sum(factor * separation[axis_k], axis=2)]
    gather x67 -> x0, local copies, waits for them, and re-layouts: 463 us -> none  [the longest x1 194 us: local(): sphere_key = frag_key[sphere_frag]]
    scatter-add x33 -> x0, other arithmetic: 305 us -> none  [the longest x1 217 us: local(): jax.ops.segment_sum(loads.T, sphere_frag.reshape(-1), num_segments=held)]
    pallas_call x0 -> x3, Pallas kernels: none -> 275 us  [the longest x1 268 us: forces(): pl.pallas_call(tiles_kernel, in_specs=[SMEM, VMEM, VMEM, VMEM], out_specs...]
where the time goes in v1:
time: 364 us; the launch traced here: 366 us
  Pallas kernels  275 us (76%)
  waiting for transfers between devices  39.9 us (11%)
  starting transfers between devices  38.5 us (11%)
  local copies, waits for them, and re-layouts  6.21 us (2%)
  other arithmetic  5.55 us (2%)
    pallas_call x1, Pallas kernels, forces(): pl.pallas_call(tiles_kernel, in_specs=[SMEM, VMEM, VMEM, VMEM], out_specs...  268 us
    all_to_all x1, starting transfers between devices, local(): lax.all_to_all(outbox, ('gx', 'gy', 'gz'), split_axis=1, concat_axis=1, t...  23.6 us
    ppermute x3, waiting for transfers between devices, with_halo(): before = lax.ppermute(last, axis, up)  17.5 us
    all_to_all x1, waiting for transfers between devices, local(): lax.all_to_all(outbox, ('gx', 'gy', 'gz'), split_axis=1, concat_axis=1, t...  9.96 us
    all_to_all x1, waiting for transfers between devices, local(): lax.all_to_all(reply, ('gx', 'gy', 'gz'), split_axis=1, concat_axis=1, ti...  9.96 us
  transfers between devices with their start and end apart: 8, of which 7 were waited for; matrix products, arithmetic and copies ran while one was open for 0% of the time, Pallas kernels for 0%

profile of v1, /device:TPU:1, one launch (start us, length us, event | category | flops | bytes accessed | tf_op | source)
XLA Modules:
  0.0 366.1 jit_solution(2978875036584931178)
XLA Ops:
  0.6 0.7 add_convert_fusion.1
  1.8 3.5 pack.1
  5.3 1.2 fusion.8
  6.5 4.2 %collective-permute-start = (f32[1,4,16,8,128]{4,3,2,1,0:T(8,128)S(1)}, f32[1,4,16,8,128]{4,3,2,1,0:T(8,128)S(1)}, u32[]{:S(2)}, u32[]{:S(2)}) collective-permute-start(f32[1,4,16,8,128]{4,3,2,1,0:T(8,128)S(1)} %bitcast.53), channel_id=1, source_target_pairs={{0,32},{32,64},{64,96},{96,0},{1,33},{33,65},{65,97},{97,1},{2,34}... | collective-permute-start | bytes 786440 | tf_op jit(solution)/shard_map/ppermute | solution.py:300
  10.7 5.4 %collective-permute-done = f32[1,4,16,8,128]{4,3,2,1,0:T(8,128)S(1)} collective-permute-done((f32[1,4,16,8,128]{4,3,2,1,0:T(8,128)S(1)}, f32[1,4,16,8,128]{4,3,2,1,0:T(8,128)S(1)}, u32[]{:S(2)}, u32[]{:S(2)}) %collective-permute-start) | collective-permute-done | bytes 262176 | tf_op jit(solution)/shard_map/ppermute | solution.py:300
  16.1 1.9 collective-permute-done.1
  18.0 1.1 pad_maximum_fusion.3
  19.1 1.4 collective-permute-start.2
  20.5 1.5 collective-permute-start.3
  22.3 8.5 %collective-permute-done.2 = f32[6,1,16,8,128]{4,3,2,1,0:T(8,128)S(1)} collective-permute-done((f32[6,1,16,8,128]{4,3,2,1,0:T(8,128)S(1)}, f32[6,1,16,8,128]{4,3,2,1,0:T(8,128)S(1)}, u32[]{:S(2)}, u32[]{:S(2)}) %collective-permute-start.2) | collective-permute-done | bytes 393248 | tf_op jit(solution)/shard_map/ppermute | solution.py:300
  31.5 1.7 collective-permute-start.4
  33.2 2.0 collective-permute-start.5
  35.2 3.5 collective-permute-done.4
  38.7 1.7 pad_maximum_fusion
  40.4 267.8 %forces.1 = f32[8,128]{1,0:T(8,128)} custom-call(s32[2048]{0:T(1024)} %bitcast.57, f32[5184,128]{1,0:T(8,128)} %bitcast.42, f32[3,256,128]{2,1,0:T(8,128)} %bitcast.45, s32[256,128]{1,0:T(8,128)} %bitcast.48), custom_call_target="tpu_custom_call" | custom-call | tf_op jit(solution)/shard_map/forces/pallas_call | solution.py:252
  308.2 0.7 maximum_bitcast_fusion
  309.0 1.3 scatter_custom_fusion
  310.4 23.6 %all-to-all-start = ((f32[7,128,2]{0,2,1:T(2,128)}), f32[7,128,2]{0,2,1:T(2,128)S(1)}, u32[]{:S(2)}, u32[]{:S(2)}) async-start(f32[7,128,2]{0,2,1:T(2,128)} %bitcast.15), calls=%async_computation | async-start | bytes 262144 | tf_op jit(solution)/shard_map/all_to_all | solution.py:331
  334.0 10.0 %all-to-all-done = f32[7,128,2]{0,2,1:T(2,128)S(1)} async-done(((f32[7,128,2]{0,2,1:T(2,128)}), f32[7,128,2]{0,2,1:T(2,128)S(1)}, u32[]{:S(2)}, u32[]{:S(2)}) %all-to-all-start) | async-done | bytes 7200 | tf_op jit(solution)/shard_map/all_to_all | solution.py:331
  345.5 0.7 gather_fusion
  346.2 0.9 broadcast_select_fusion
  347.1 4.1 %all-to-all-start.1 = ((f32[6,128,2]{0,2,1:T(2,128)}), f32[6,128,2]{0,2,1:T(2,128)S(1)}, u32[]{:S(2)}, u32[]{:S(2)}) async-start(f32[6,128,2]{0,2,1:T(2,128)} %broadcast_select_fusion), calls=%async_computation.1 | async-start | bytes 262144 | tf_op jit(solution)/shard_map/all_to_all | solution.py:340
  351.2 10.0 %all-to-all-done.1 = f32[6,128,2]{0,2,1:T(2,128)S(1)} async-done(((f32[6,128,2]{0,2,1:T(2,128)}), f32[6,128,2]{0,2,1:T(2,128)S(1)}, u32[]{:S(2)}, u32[]{:S(2)}) %all-to-all-start.1) | async-done | bytes 6176 | tf_op jit(solution)/shard_map/all_to_all | solution.py:340
  362.5 3.6 move.1
  (45 shorter events, 4.4 us)
Async XLA Ops:
  1.8 20.2 %copy-start.2 = (s32[64,1]{0,1:T(1,128)S(1)}, s32[64,1]{0,1:T(1,128)}, u32[]{:S(2)}) copy-start(s32[64,1]{0,1:T(1,128)} %param.13) | copy-start | bytes 772
  5.3 26.2 %copy-start = (f32[2048,128]{1,0:T(8,128)S(1)}, f32[2048,128]{1,0:T(8,128)}, u32[]{:S(2)}) copy-start(f32[2048,128]{1,0:T(8,128)} %pack.1) | copy-start | bytes 3145732
  6.5 28.7 %copy-start.6 = (f32[48]{0:T(128)S(1)}, f32[48]{0:T(128)}, u32[]{:S(2)}) copy-start(f32[48]{0:T(128)} %param.18) | copy-start | bytes 580
  6.5 9.6 %collective-permute-start = (f32[1,4,16,8,128]{4,3,2,1,0:T(8,128)S(1)}, f32[1,4,16,8,128]{4,3,2,1,0:T(8,128)S(1)}, u32[]{:S(2)}, u32[]{:S(2)}) collective-permute-start(f32[1,4,16,8,128]{4,3,2,1,0:T(8,128)S(1)} %bitcast.53), channel_id=1, source_target_pairs={{0,32},{32,64},{64,96},{96,0},{1,33},{33,65},{65,97},{97,1},{2,34}... | collective-permute-start | bytes 786440 | tf_op jit(solution)/shard_map/ppermute | solution.py:300
  10.7 7.3 %collective-permute-start.1 = (f32[1,4,16,8,128]{4,3,2,1,0:T(8,128)S(1)}, f32[1,4,16,8,128]{4,3,2,1,0:T(8,128)S(1)}, u32[]{:S(2)}, u32[]{:S(2)}) collective-permute-start(f32[1,4,16,8,128]{4,3,2,1,0:T(8,128)S(1)} %bitcast.52), channel_id=1, source_target_pairs={{32,0},{64,32},{96,64},{0,96},{33,1},{65,33},{97,65},{1,97},{34,2}... | collective-permute-start | bytes 786440 | tf_op jit(solution)/shard_map/ppermute | solution.py:301
  19.1 11.8 %collective-permute-start.2 = (f32[6,1,16,8,128]{4,3,2,1,0:T(8,128)S(1)}, f32[6,1,16,8,128]{4,3,2,1,0:T(8,128)S(1)}, u32[]{:S(2)}, u32[]{:S(2)}) collective-permute-start(f32[6,1,16,8,128]{4,3,2,1,0:T(8,128)S(1)} %get-tuple-element.6), channel_id=1, source_target_pairs={{0,8},{8,16},{16,24},{24,0},{1,9},{9,17},{17,25},{25,1},{2,10},{10... | collective-permute-start | bytes 1179656 | tf_op jit(solution)/shard_map/ppermute | solution.py:300
  20.5 11.0 %collective-permute-start.3 = (f32[6,1,16,8,128]{4,3,2,1,0:T(8,128)S(1)}, f32[6,1,16,8,128]{4,3,2,1,0:T(8,128)S(1)}, u32[]{:S(2)}, u32[]{:S(2)}) collective-permute-start(f32[6,1,16,8,128]{4,3,2,1,0:T(8,128)S(1)} %get-tuple-element.7), channel_id=1, source_target_pairs={{8,0},{16,8},{24,16},{0,24},{9,1},{17,9},{25,17},{1,25},{10,2},{18... | collective-permute-start | bytes 1179656 | tf_op jit(solution)/shard_map/ppermute | solution.py:301
  31.5 7.2 %collective-permute-start.4 = (f32[6,6,1,8,128]{4,3,2,1,0:T(8,128)S(1)}, f32[6,6,1,8,128]{4,3,2,1,0:T(8,128)S(1)}, u32[]{:S(2)}, u32[]{:S(2)}) collective-permute-start(f32[6,6,1,8,128]{4,3,2,1,0:T(8,128)S(1)} %get-tuple-element.4), channel_id=1, source_target_pairs={{0,1},{1,2},{2,3},{3,4},{4,5},{5,6},{6,7},{7,0},{8,9},{9,10},{10,1... | collective-permute-start | bytes 442376 | tf_op jit(solution)/shard_map/ppermute | solution.py:300
  33.2 5.5 %collective-permute-start.5 = (f32[6,6,1,8,128]{4,3,2,1,0:T(8,128)S(1)}, f32[6,6,1,8,128]{4,3,2,1,0:T(8,128)S(1)}, u32[]{:S(2)}, u32[]{:S(2)}) collective-permute-start(f32[6,6,1,8,128]{4,3,2,1,0:T(8,128)S(1)} %get-tuple-element.5), channel_id=1, source_target_pairs={{1,0},{2,1},{3,2},{4,3},{5,4},{6,5},{7,6},{0,7},{9,8},{10,9},{11,1... | collective-permute-start | bytes 442376 | tf_op jit(solution)/shard_map/ppermute | solution.py:301
  40.4 304.7 %copy-start.3 = (f32[6,48]{1,0:T(8,128)S(1)}, f32[6,48]{1,0:T(8,128)}, u32[]{:S(2)}) copy-start(f32[6,48]{1,0:T(8,128)} %param.16) | copy-start | bytes 3460
  40.4 304.7 %copy-start.4 = (f32[48]{0:T(128)S(1)}, f32[48]{0:T(128)}, u32[]{:S(2)}) copy-start(f32[48]{0:T(128)} %param.17) | copy-start | bytes 580
  40.4 304.7 %copy-start.5 = (f32[3]{0:T(128)S(1)}, f32[3]{0:T(128)}, u32[]{:S(2)}) copy-start(f32[3]{0:T(128)} %constant.65) | copy-start | bytes 40
  310.4 33.5 %all-to-all-start = ((f32[7,128,2]{0,2,1:T(2,128)}), f32[7,128,2]{0,2,1:T(2,128)S(1)}, u32[]{:S(2)}, u32[]{:S(2)}) async-start(f32[7,128,2]{0,2,1:T(2,128)} %bitcast.15), calls=%async_computation | async-start | bytes 262144 | tf_op jit(solution)/shard_map/all_to_all | solution.py:331
  345.2 20.8 %copy-start.1 = (f32[6,48]{1,0:T(8,128)}, f32[6,48]{1,0:T(8,128)S(1)}, u32[]{:S(2)}) copy-start(f32[6,48]{1,0:T(8,128)S(1)} %pad_maximum_fusion.9) | copy-start | bytes 3460
  347.1 14.1 %all-to-all-start.1 = ((f32[6,128,2]{0,2,1:T(2,128)}), f32[6,128,2]{0,2,1:T(2,128)S(1)}, u32[]{:S(2)}, u32[]{:S(2)}) async-start(f32[6,128,2]{0,2,1:T(2,128)} %broadcast_select_fusion), calls=%async_computation.1 | async-start | bytes 262144 | tf_op jit(solution)/shard_map/all_to_all | solution.py:340

commit v2 on v1

v2 whole, which is shorter than its diff:
```python
import functools

import jax
import jax.numpy as jnp
from jax import lax
from jax.experimental import pallas as pl
from jax.experimental.pallas import tpu as pltpu
from jax.sharding import PartitionSpec as P

CAP = 2
QUICK = 6
GROUP = 8
REACH = 0.14001
time_step = 0.01
gravity = 9.81
epsilon_sq = 1e-08
VMEM = pl.BlockSpec(memory_space=pltpu.VMEM)


def lane_take(rows, index):
    return jnp.take_along_axis(rows, index, axis=1, mode="promise_in_bounds")


def cross_rows(first, second):
    return [
        first[1] * second[2] - first[2] * second[1],
        first[2] * second[0] - first[0] * second[2],
        first[0] * second[1] - first[1] * second[0],
    ]


def pack_kernel(state, frag, table, out):
    keys = jnp.broadcast_to(table[...], (8, 128))
    for g in range(frag.shape[0] // 8):
        rows = pl.ds(8 * g, 8)
        for k in range(7):
            out[pl.ds(64 * g + k, 8, stride=8), :] = state[k, rows, :]
        out[pl.ds(64 * g + 7, 8, stride=8), :] = lane_take(keys, frag[rows, :])


def tiles_kernel(
    codes, cells, arms, frag, out, cand, mask, counts, where_v, where_s, place_v, place_s, lens_v, lens_s, items,
    carry, lists, shifts, wide_a, wide_b, push_x, push_y, push_z, loads, sems,
):
    pushes = (push_x, push_y, push_z)
    lines = codes.shape[0]
    tiles = lines * 128
    pad = cells.shape[0] // 8
    ny, nz = 6, 18
    owned = 256
    depth = lists.shape[0] // (8 * owned)
    sub = lax.broadcasted_iota(jnp.int32, (8, 128), 0)
    lane = lax.broadcasted_iota(jnp.int32, (8, 128), 1)

    code = codes[...]
    own_of = (code * 38837) >> 20
    way = code - 27 * own_of
    step_x = ((way * 57) >> 9) - 1
    left = way - 9 * (step_x + 1)
    step_y = ((left * 11) >> 5) - 1
    step_z = left - 3 * (step_y + 1) - 1
    cell_of = ((own_of >> 6) + 1 + step_x) * (ny * nz) + (((own_of >> 4) & 3) + 1 + step_y) * nz
    cell_of = cell_of + (own_of & 15) + 1 + step_z
    where_v[...] = cell_of * 8 + (way << 16)
    place_v[...] = own_of
    first_copy = pltpu.make_async_copy(where_v, where_s, sems.at[0])
    first_copy.start()

    @pl.loop(0, pad // 8)
    def _(g):
        base = pl.multiple_of(g * 64, 64)
        pos = [cells[pl.ds(base + k, 8, stride=8), :] for k in range(3)]
        reach = cells[pl.ds(base + 6, 8, stride=8), :] + REACH
        reach = reach * reach
        near = [p * p for p in pos]
        far = [(1.0 - p) * (1.0 - p) for p in pos]
        bits = jnp.full((8, 128), 1 << 13, jnp.int32)
        for o in range(27):
            steps = (o // 9 - 1, o // 3 % 3 - 1, o % 3 - 1)
            terms = [near[k] if s > 0 else far[k] for k, s in enumerate(steps) if s]
            if not terms:
                continue
            bits = bits | jnp.where(sum(terms[1:], terms[0]) <= reach, 1 << o, 0)
        cand[pl.ds(pl.multiple_of(g * 8, 8), 8), :] = bits

    @pl.loop(0, 27)
    def _(o):
        step_x = ((o * 57) >> 9) - 1
        left = o - 9 * (step_x + 1)
        step_y = ((left * 11) >> 5) - 1
        step_z = left - 3 * (step_y + 1) - 1
        value = jnp.where(sub == 0, step_x, jnp.where(sub == 1, step_y, jnp.where(sub == 2, step_z, 0)))
        shifts[pl.ds(pl.multiple_of(o * 8, 8), 8), :] = value.astype(jnp.float32)

    @pl.loop(0, owned // 16)
    def _(b):
        rows = pl.ds(pl.multiple_of(b * 128, 128), 128)
        for push in pushes:
            push[rows, :] = jnp.zeros((128, 128), jnp.float32)

    first_copy.wait()

    @pl.loop(0, tiles // 16)
    def _(b):
        line, at = b >> 3, (b & 7) * 16
        for u in range(16):
            word = where_s[line, at + u]
            mask[pl.ds(b * 16 + u, 1), :] = (cand[pl.ds((word & 0xFFFF) >> 3, 1), :] >> (word >> 16)) & 1

    row = lax.broadcasted_iota(jnp.int32, (128, 128), 0)
    col = lax.broadcasted_iota(jnp.int32, (128, 128), 1)
    before = (row < col).astype(jnp.bfloat16)
    ones = jnp.ones((8, 128), jnp.bfloat16)

    @pl.loop(0, lines)
    def _(b):
        rows = pl.ds(pl.multiple_of(b * 128, 128), 128)
        active = mask[rows, :]
        flags = active.astype(jnp.float32).astype(jnp.bfloat16)
        rank = jnp.dot(flags, before, preferred_element_type=jnp.float32).astype(jnp.int32)
        number = lax.dot_general(ones, flags, (((1,), (1,)), ((), ())), preferred_element_type=jnp.float32)
        counts[pl.ds(b, 1), :] = number[0:1]
        value = jnp.where(active > 0, ((col - rank) << 7) | col, 0)
        for bit in range(7):
            moved = pltpu.roll(value, 128 - (1 << bit), axis=1)
            flag = 1 << (7 + bit)
            value = jnp.where((moved & flag) != 0, moved, jnp.where((value & flag) != 0, 0, value))
        mask[rows, :] = value & 127

    both = jnp.concatenate([before, jnp.ones((128, 128), jnp.bfloat16)], axis=1)
    cell_id = lax.broadcasted_iota(jnp.int32, (owned, 128), 0)
    carry[...] = jnp.zeros((owned, 128), jnp.float32)

    @pl.loop(0, lines)
    def _(b):
        mine = place_v[pl.ds(b, 1), :]
        hot = cell_id == mine
        amount = jnp.where(hot, counts[pl.ds(b, 1), :], 0.0)
        summed = jnp.dot(amount.astype(jnp.bfloat16), both, preferred_element_type=jnp.float32)
        so_far = carry[...]
        at = jnp.sum(jnp.where(hot, summed[:, 0:128] + so_far, 0.0), axis=0, keepdims=True)
        carry[...] = so_far + summed[:, 128:256]
        place_v[pl.ds(b, 1), :] = mine * (depth * 128) + at.astype(jnp.int32)

    length = carry[...].T[0:8, :]
    most = jnp.max(length, axis=1, keepdims=True)
    lens_v[...] = jnp.where(lax.broadcasted_iota(jnp.int32, (8, owned), 0) == 0, length, most).astype(jnp.int32)
    copies = [
        pltpu.make_async_copy(place_v, place_s, sems.at[1]),
        pltpu.make_async_copy(lens_v, lens_s, sems.at[2]),
    ]
    for copy in copies:
        copy.start()
    for copy in copies:
        copy.wait()

    def append(sorted_rows, spot):
        turn = spot & 127
        to = pl.multiple_of((spot >> 7) * 8, 8)
        turned = pltpu.roll(sorted_rows, turn, axis=1)
        pltpu.store(lists.at[pl.ds(to, 8), :], turned, mask=lane >= turn)
        lists[pl.ds(to + 8, 8), :] = turned

    @pl.loop(0, tiles // 16)
    def _(b):
        line, at = b >> 3, (b & 7) * 16
        for u in range(16):
            word = where_s[line, at + u]
            values = cells[pl.ds(pl.multiple_of(word & 0xFFFF, 8), 8), :]
            index = jnp.broadcast_to(mask[pl.ds(b * 16 + u, 1), :], (8, 128))
            shift = shifts[pl.ds(pl.multiple_of((word >> 16) * 8, 8), 8), :]
            append(lane_take(values, index) + shift, place_s[line, at + u])

    dummy = jnp.where(sub < 3, 1000.0, 0.1)

    def item(c, k):
        return (c << 16) | (c * (2 * depth) + k)

    def close(b, total):
        for u in range(8):
            c = b * 8 + u
            length = lens_s[0, c]
            append(dummy, c * (depth * 128) + length)
            for k in range(QUICK):
                items[total + k] = item(c, k)
            total = total + jnp.minimum((length + 63) >> 6, QUICK)
        return total

    number = lax.fori_loop(0, owned // 8, close, 0)

    def longer(c, total):
        def add(k, total):
            items[total] = item(c, k)
            return total + 1

        return lax.fori_loop(QUICK, (lens_s[0, c] + 63) >> 6, add, total)

    longest = lens_s[1, 0]
    number = lax.fori_loop(0, jnp.where(longest > 64 * QUICK, owned, 0), longer, number)
    for k in range(3 * GROUP):
        items[number + k] = owned << 16

    which_row = lax.broadcasted_iota(jnp.int32, (24, 1024), 0)
    which_col = lax.broadcasted_iota(jnp.int32, (24, 1024), 1)
    pick = ((which_row & 7) == (which_col >> 7)).astype(jnp.float32).astype(jnp.bfloat16)

    def spread(words, wide):
        splits = []
        for word in words:
            spot = word & 0xFFFF
            values = lists[pl.ds(pl.multiple_of((spot >> 1) * 8, 8), 8), :]
            values = pltpu.roll(values, (spot & 1) * 64, axis=1)
            high = values.astype(jnp.bfloat16).astype(jnp.float32)
            rest = values - high
            mid = rest.astype(jnp.bfloat16).astype(jnp.float32)
            split = jnp.concatenate([high, mid, rest - mid], axis=0)
            splits.append(split.T[0:64])
        split = jnp.concatenate(splits, axis=0).astype(jnp.bfloat16)
        spreads = jnp.dot(split, pick, preferred_element_type=jnp.float32)
        for u in range(8 * len(words)):
            for k in range(8):
                wide[8 * u + k] = spreads[8 * u : 8 * u + 8, 128 * k : 128 * k + 128]

    def press(word, wide, first):
        c = word >> 16
        base = ((c >> 6) + 1) * (ny * nz) + (((c >> 4) & 3) + 1) * nz + (c & 15) + 1
        own = [jnp.broadcast_to(cells[pl.ds(base * 8 + k, 1), :], (8, 128)) for k in range(8)]
        total = [None] * 3
        for u in range(8):
            other = [wide[8 * (first + u) + k] for k in range(8)]
            apart = [other[k] - own[k] for k in range(3)]
            square = apart[0] * apart[0] + apart[1] * apart[1] + apart[2] * apart[2] + epsilon_sq
            inverse = lax.rsqrt(square)
            reach = own[6] + other[6]
            depth_in = jnp.where(own[7] != other[7], jnp.maximum(reach - square * inverse, 0.0), 0.0)
            closing = (
                (other[3] - own[3]) * apart[0] + (other[4] - own[4]) * apart[1] + (other[5] - own[5]) * apart[2]
            )
            along = closing * inverse - 50.0 * depth_in
            area = own[6] * other[6] * depth_in
            factor = area * lax.rsqrt(jnp.maximum(area * reach, 1e-20)) * along * inverse
            for k in range(3):
                term = factor * apart[k]
                total[k] = term if u == 0 else total[k] + term
        rows = pl.ds(pl.multiple_of(c * 8, 8), 8)
        for k in range(3):
            pushes[k][rows, :] += total[k]

    def group(n):
        return [items[n * GROUP + k] for k in range(GROUP)]

    spread(group(0), wide_a)

    @pl.loop(0, (number + (2 * GROUP - 1)) // (2 * GROUP))
    def _(p):
        def half(n, now, later):
            spread(group(n + 1), later)
            for k, word in enumerate(group(n)):
                press(word, now, 8 * k)

        half(2 * p, wide_a, wide_b)
        half(2 * p + 1, wide_b, wide_a)

    ids = lax.broadcasted_iota(jnp.int32, (64, 128), 0)

    def gather(g, total):
        rows = pl.ds(pl.multiple_of(g * 8, 8), 8)
        force = []
        for push in pushes:
            parts = [push[pl.ds(g * 64 + s, 8, stride=8), :] for s in range(8)]
            while len(parts) > 1:
                parts = [parts[i] + parts[i + 1] for i in range(0, len(parts), 2)]
            force.append(2.0 * parts[0])
        turn = cross_rows([arms[k, rows, :] for k in range(3)], force)
        zero = jnp.zeros((8, 128), jnp.float32)
        for k, value in enumerate(force + turn + [zero, zero]):
            loads[pl.ds(k, 8, stride=8), :] = value
        wide = jnp.concatenate([loads[pl.ds(8 * c, 8), :] for c in range(8)], axis=1)
        high = wide.astype(jnp.bfloat16).astype(jnp.float32)
        rest = wide - high
        mid = rest.astype(jnp.bfloat16).astype(jnp.float32)
        split = jnp.concatenate([high, mid, rest - mid], axis=0).astype(jnp.bfloat16)
        which = jnp.concatenate(
            [(ids == frag[pl.ds(g * 8 + c, 1), :]).astype(jnp.float32) for c in range(8)], axis=1
        ).astype(jnp.bfloat16)
        return total + lax.dot_general(split, which, (((1,), (1,)), ((), ())), preferred_element_type=jnp.float32)

    total = lax.fori_loop(0, owned // 8, gather, jnp.zeros((24, 64), jnp.float32))
    out[...] = total[0:8] + total[8:16] + total[16:24]


def move_kernel(state, arms, frag, table, out):
    rows_of = [jnp.broadcast_to(table[k : k + 1, :], (8, 128)) for k in range(6)]
    for g in range(frag.shape[0] // 8):
        rows = pl.ds(8 * g, 8)
        index = frag[rows, :]
        motion = [lane_take(r, index) for r in rows_of]
        velocity, spin = motion[0:3], motion[3:6]
        lever = [arms[k, rows, :] for k in range(3)]
        half = [0.5 * time_step * w for w in spin]
        turned = cross_rows(half, lever)
        twice = cross_rows(half, turned)
        scale = 2.0 / (1.0 + half[0] * half[0] + half[1] * half[1] + half[2] * half[2])
        moved = [lever[k] + scale * (turned[k] + twice[k]) for k in range(3)]
        swing = cross_rows(spin, moved)
        for k in range(3):
            out[k, rows, :] = state[k, rows, :] + time_step * velocity[k] + (moved[k] - lever[k])
            out[3 + k, rows, :] = velocity[k] + swing[k]


def pack(state, frag, table):
    n = frag.shape[0]
    part = n // 4
    return pl.pallas_call(
        pack_kernel,
        grid=(4,),
        in_specs=[
            pl.BlockSpec((7, part, 128), lambda i: (0, i, 0)),
            pl.BlockSpec((part, 128), lambda i: (i, 0)),
            pl.BlockSpec((1, 128), lambda i: (0, 0)),
        ],
        out_specs=pl.BlockSpec((8 * part, 128), lambda i: (i, 0)),
        out_shape=jax.ShapeDtypeStruct((8 * n, 128), jnp.float32),
        name="pack",
    )(state, frag, table)


def forces(codes, cells, arms, frag):
    lines = codes.shape[0] // 128
    owned, depth = frag.shape[0], 29
    return pl.pallas_call(
        tiles_kernel,
        in_specs=[VMEM, VMEM, VMEM, VMEM],
        out_specs=VMEM,
        out_shape=jax.ShapeDtypeStruct((8, 64), jnp.float32),
        scratch_shapes=[
            pltpu.VMEM((cells.shape[0] // 8, 128), jnp.int32),
            pltpu.VMEM((lines * 128, 128), jnp.int32),
            pltpu.VMEM((lines, 128), jnp.float32),
            pltpu.VMEM((lines, 128), jnp.int32),
            pltpu.SMEM((lines, 128), jnp.int32),
            pltpu.VMEM((lines, 128), jnp.int32),
            pltpu.SMEM((lines, 128), jnp.int32),
            pltpu.VMEM((8, owned), jnp.int32),
            pltpu.SMEM((8, owned), jnp.int32),
            pltpu.SMEM((owned * 54 + 32,), jnp.int32),
            pltpu.VMEM((owned, 128), jnp.float32),
            pltpu.VMEM((owned * depth * 8, 128), jnp.float32),
            pltpu.VMEM((27 * 8, 128), jnp.float32),
            pltpu.VMEM((64 * GROUP, 8, 128), jnp.float32),
            pltpu.VMEM((64 * GROUP, 8, 128), jnp.float32),
            pltpu.VMEM((owned * 8 + 8, 128), jnp.float32),
            pltpu.VMEM((owned * 8 + 8, 128), jnp.float32),
            pltpu.VMEM((owned * 8 + 8, 128), jnp.float32),
            pltpu.VMEM((64, 128), jnp.float32),
            pltpu.SemaphoreType.DMA((3,)),
        ],
        compiler_params=pltpu.CompilerParams(vmem_limit_bytes=60 * 1024 * 1024),
        name="forces",
    )(codes.reshape(lines, 128), cells, arms, frag)


def move(state, arms, frag, table):
    n = frag.shape[0]
    part = n // 4
    return pl.pallas_call(
        move_kernel,
        grid=(4,),
        in_specs=[
            pl.BlockSpec((3, part, 128), lambda i: (0, i, 0)),
            pl.BlockSpec((3, part, 128), lambda i: (0, i, 0)),
            pl.BlockSpec((part, 128), lambda i: (i, 0)),
            pl.BlockSpec((8, 128), lambda i: (0, 0)),
        ],
        out_specs=pl.BlockSpec((6, part, 128), lambda i: (0, i, 0)),
        out_shape=jax.ShapeDtypeStruct((6, n, 128), jnp.float32),
        name="move",
    )(state, arms, frag, table)


def with_halo(x, sides):
    for axis, dim in sides:
        devices, length = (lax.axis_size(axis), x.shape[dim])
        up = [(i, (i + 1) % devices) for i in range(devices)]
        down = [(j, i) for i, j in up]
        last = lax.slice_in_dim(x, length - 1, length, axis=dim)
        initial = lax.slice_in_dim(x, 0, 1, axis=dim)
        before = lax.ppermute(last, axis, up)
        after = lax.ppermute(initial, axis, down)
        x = jnp.concatenate([before, x, after], axis=dim)
    return x


def advance(motion, sums, inv_mass, inv_moment):
    pull = jnp.array([0.0, 0.0, gravity], jnp.float32)[:, None]
    velocity = motion[0:3] + time_step * (sums[0:3] * inv_mass[None, :] - pull)
    spin = motion[3:6] + time_step * sums[3:6] * inv_moment[None, :]
    return jnp.concatenate([velocity, spin], axis=0)


def local(state, arms, sphere_frag, frag_owner, frag_clump, tiles, clump_motion, inv_mass, inv_moment):
    cx, cy, cz, slots = state.shape[1:]
    count = cx * cy * cz
    owned = inv_mass.shape[0]
    held = frag_clump.shape[0]
    bricks = lax.axis_size("gx") * lax.axis_size("gy") * lax.axis_size("gz")
    owner = frag_owner[:, 0]
    frag = sphere_frag.reshape(count, slots)
    key = (owner * owned + frag_clump).astype(jnp.float32)
    own_cells = pack(state.reshape(7, count, slots), frag, jnp.pad(key, (0, 128 - held))[None])
    padded = with_halo(own_cells.reshape(cx, cy, cz, 8, slots), (("gx", 0), ("gy", 1), ("gz", 2)))
    frag_sums = forces(tiles[0], padded.reshape(-1, slots), arms.reshape(3, count, slots), frag)[0:6]

    hits = (owner[:, None] == jnp.arange(bricks, dtype=jnp.int32)[None, :]).astype(jnp.int32)
    rank = jnp.sum((jnp.cumsum(hits, axis=0) - hits) * hits, axis=1)
    slot_index = owner * CAP + rank
    payload = jnp.concatenate([frag_sums, (frag_clump + 1).astype(jnp.float32)[None]], axis=0)
    outbox = jnp.zeros((7, bricks * CAP), jnp.float32).at[:, slot_index].set(payload)
    inbox = lax.all_to_all(outbox, ("gx", "gy", "gz"), split_axis=1, concat_axis=1, tiled=True)
    labels = (jnp.arange(owned, dtype=jnp.int32) + 1).astype(jnp.float32)
    which = (inbox[6][:, None] == labels[None, :]).astype(jnp.float32)
    clump_sums = jnp.dot(
        inbox[0:6], which, precision=lax.Precision.HIGHEST, preferred_element_type=jnp.float32
    )
    clump_next = advance(clump_motion, clump_sums, inv_mass, inv_moment)
    column = jnp.clip(inbox[6].astype(jnp.int32) - 1, 0, owned - 1)
    reply = jnp.take(clump_next, column, axis=1)
    answer = lax.all_to_all(reply, ("gx", "gy", "gz"), split_axis=1, concat_axis=1, tiled=True)
    frag_motion = jnp.take(answer, slot_index, axis=1)
    table = jnp.pad(frag_motion, ((0, 2), (0, 128 - held)))
    sphere_next = move(state.reshape(7, count, slots), arms.reshape(3, count, slots), frag, table)
    return sphere_next.reshape(6, cx, cy, cz, slots), clump_next


def solution(mesh):
    return jax.shard_map(
        local,
        mesh=mesh,
        in_specs=(
            P(None, "gx", "gy", "gz", None),
            P(None, "gx", "gy", "gz", None),
            P("gx", "gy", "gz", None),
            P(("gx", "gy", "gz"), None),
            P(("gx", "gy", "gz")),
            P(("gx", "gy", "gz"), None),
            P(None, ("gx", "gy", "gz")),
            P(("gx", "gy", "gz")),
            P(("gx", "gy", "gz")),
        ),
        out_specs=(P(None, "gx", "gy", "gz", None), P(None, ("gx", "gy", "gz"))),
        check_vma=False,
    )
```

time: 364 us -> 195 us (0.54)
  Pallas kernels: 275 us -> 115 us
  starting transfers between devices: 38.5 us -> 27.2 us
    pallas_call x1, Pallas kernels: 268 us -> 108 us  [forces(): pl.pallas_call(tiles_kernel, in_specs=[VMEM, VMEM, VMEM, VMEM], out_specs...]
    all_to_all x1, starting transfers between devices: 23.6 us -> 12.3 us  [local(): lax.all_to_all(outbox, ('gx', 'gy', 'gz'), split_axis=1, concat_axis=1, t...]
where the time goes in v2:
time: 195 us
  Pallas kernels  115 us (59%)
  waiting for transfers between devices  39.9 us (20%)
  starting transfers between devices  27.2 us (14%)
  local copies, waits for them, and re-layouts  6.21 us (3%)
  other arithmetic  5.55 us (3%)
    pallas_call x1, Pallas kernels, forces(): pl.pallas_call(tiles_kernel, in_specs=[VMEM, VMEM, VMEM, VMEM], out_specs...  108 us
    ppermute x3, waiting for transfers between devices, with_halo(): before = lax.ppermute(last, axis, up)  17.5 us
    all_to_all x1, starting transfers between devices, local(): lax.all_to_all(outbox, ('gx', 'gy', 'gz'), split_axis=1, concat_axis=1, t...  12.3 us
    all_to_all x1, waiting for transfers between devices, local(): lax.all_to_all(outbox, ('gx', 'gy', 'gz'), split_axis=1, concat_axis=1, t...  9.96 us
    all_to_all x1, waiting for transfers between devices, local(): lax.all_to_all(reply, ('gx', 'gy', 'gz'), split_axis=1, concat_axis=1, ti...  9.96 us
    ppermute x3, starting transfers between devices, with_halo(): before = lax.ppermute(last, axis, up)  7.26 us
    all_to_all x1, starting transfers between devices, local(): lax.all_to_all(reply, ('gx', 'gy', 'gz'), split_axis=1, concat_axis=1, ti...  4.13 us
  transfers between devices with their start and end apart: 8, of which 7 were waited for; matrix products, arithmetic and copies ran while one was open for 0% of the time, Pallas kernels for 0%

profile of v2, /device:TPU:1, one launch (start us, length us, event | category | flops | bytes accessed | tf_op | source)
XLA Modules:
  0.0 195.3 jit_solution(8311020642458733350)
XLA Ops:
  0.6 0.7 add_convert_fusion.1
  1.8 3.5 %pack.1 = f32[2048,128]{1,0:T(8,128)} custom-call(f32[7,256,128]{2,1,0:T(8,128)} %bitcast.43, s32[256,128]{1,0:T(8,128)} %bitcast.47, f32[1,128]{1,0:T(1,128)} %pad_bitcast_fusion.table), custom_call_target="tpu_custom_call" | custom-call | tf_op jit(solution)/shard_map/pack/pallas_call | solution.py:314
  5.3 1.2 fusion.8
  6.5 4.2 %collective-permute-start = (f32[1,4,16,8,128]{4,3,2,1,0:T(8,128)S(1)}, f32[1,4,16,8,128]{4,3,2,1,0:T(8,128)S(1)}, u32[]{:S(2)}, u32[]{:S(2)}) collective-permute-start(f32[1,4,16,8,128]{4,3,2,1,0:T(8,128)S(1)} %bitcast.53), channel_id=1, source_target_pairs={{0,32},{32,64},{64,96},{96,0},{1,33},{33,65},{65,97},{97,1},{2,34}... | collective-permute-start | bytes 786440 | tf_op jit(solution)/shard_map/ppermute | solution.py:388
  10.7 5.4 %collective-permute-done = f32[1,4,16,8,128]{4,3,2,1,0:T(8,128)S(1)} collective-permute-done((f32[1,4,16,8,128]{4,3,2,1,0:T(8,128)S(1)}, f32[1,4,16,8,128]{4,3,2,1,0:T(8,128)S(1)}, u32[]{:S(2)}, u32[]{:S(2)}) %collective-permute-start) | collective-permute-done | bytes 262176 | tf_op jit(solution)/shard_map/ppermute | solution.py:388
  16.1 1.9 collective-permute-done.1
  18.0 1.1 pad_maximum_fusion.3
  19.1 1.4 collective-permute-start.2
  20.5 1.5 collective-permute-start.3
  22.3 8.5 %collective-permute-done.2 = f32[6,1,16,8,128]{4,3,2,1,0:T(8,128)S(1)} collective-permute-done((f32[6,1,16,8,128]{4,3,2,1,0:T(8,128)S(1)}, f32[6,1,16,8,128]{4,3,2,1,0:T(8,128)S(1)}, u32[]{:S(2)}, u32[]{:S(2)}) %collective-permute-start.2) | collective-permute-done | bytes 393248 | tf_op jit(solution)/shard_map/ppermute | solution.py:388
  31.5 1.7 collective-permute-start.4
  33.2 2.0 %collective-permute-start.5 = (f32[6,6,1,8,128]{4,3,2,1,0:T(8,128)S(1)}, f32[6,6,1,8,128]{4,3,2,1,0:T(8,128)S(1)}, u32[]{:S(2)}, u32[]{:S(2)}) collective-permute-start(f32[6,6,1,8,128]{4,3,2,1,0:T(8,128)S(1)} %get-tuple-element.5), channel_id=1, source_target_pairs={{1,0},{2,1},{3,2},{4,3},{5,4},{6,5},{7,6},{0,7},{9,8},{10,9},{11,1... | collective-permute-start | bytes 442376 | tf_op jit(solution)/shard_map/ppermute | solution.py:389
  35.2 3.5 %collective-permute-done.4 = f32[6,6,1,8,128]{4,3,2,1,0:T(8,128)S(1)} collective-permute-done((f32[6,6,1,8,128]{4,3,2,1,0:T(8,128)S(1)}, f32[6,6,1,8,128]{4,3,2,1,0:T(8,128)S(1)}, u32[]{:S(2)}, u32[]{:S(2)}) %collective-permute-start.4) | collective-permute-done | bytes 147488 | tf_op jit(solution)/shard_map/ppermute | solution.py:388
  38.7 1.7 pad_maximum_fusion
  40.4 108.3 %forces.1 = f32[8,64]{1,0:T(8,128)} custom-call(s32[16,128]{1,0:T(8,128)} %bitcast.57, f32[5184,128]{1,0:T(8,128)} %bitcast.42, f32[3,256,128]{2,1,0:T(8,128)} %bitcast.45, s32[256,128]{1,0:T(8,128)} %bitcast.48), custom_call_target="tpu_custom_call" | custom-call | tf_op jit(solution)/shard_map/forces/pallas_call | solution.py:331
  148.8 0.7 maximum_bitcast_fusion
  149.6 1.3 scatter_custom_fusion
  150.9 12.3 %all-to-all-start = ((f32[7,128,2]{0,2,1:T(2,128)}), f32[7,128,2]{0,2,1:T(2,128)S(1)}, u32[]{:S(2)}, u32[]{:S(2)}) async-start(f32[7,128,2]{0,2,1:T(2,128)} %bitcast.15), calls=%async_computation | async-start | bytes 262144 | tf_op jit(solution)/shard_map/all_to_all | solution.py:419
  163.2 10.0 %all-to-all-done = f32[7,128,2]{0,2,1:T(2,128)S(1)} async-done(((f32[7,128,2]{0,2,1:T(2,128)}), f32[7,128,2]{0,2,1:T(2,128)S(1)}, u32[]{:S(2)}, u32[]{:S(2)}) %all-to-all-start) | async-done | bytes 7200 | tf_op jit(solution)/shard_map/all_to_all | solution.py:419
  174.7 0.7 gather_fusion
  175.4 0.9 broadcast_select_fusion
  176.3 4.1 %all-to-all-start.1 = ((f32[6,128,2]{0,2,1:T(2,128)}), f32[6,128,2]{0,2,1:T(2,128)S(1)}, u32[]{:S(2)}, u32[]{:S(2)}) async-start(f32[6,128,2]{0,2,1:T(2,128)} %broadcast_select_fusion), calls=%async_computation.1 | async-start | bytes 262144 | tf_op jit(solution)/shard_map/all_to_all | solution.py:428
  180.5 10.0 %all-to-all-done.1 = f32[6,128,2]{0,2,1:T(2,128)S(1)} async-done(((f32[6,128,2]{0,2,1:T(2,128)}), f32[6,128,2]{0,2,1:T(2,128)S(1)}, u32[]{:S(2)}, u32[]{:S(2)}) %all-to-all-start.1) | async-done | bytes 6176 | tf_op jit(solution)/shard_map/all_to_all | solution.py:428
  191.7 3.6 %move.1 = f32[6,256,128]{2,1,0:T(8,128)} custom-call(f32[7,256,128]{2,1,0:T(8,128)} %bitcast.44, f32[3,256,128]{2,1,0:T(8,128)} %bitcast.46, s32[256,128]{1,0:T(8,128)} %bitcast.49, f32[8,128]{1,0:T(8,128)} %pad.9.table), custom_call_target="tpu_custom_call" | custom-call | tf_op jit(solution)/shard_map/move/pallas_call | solution.py:366
  (45 shorter events, 4.4 us)
Async XLA Ops:
  1.8 20.2 %copy-start.2 = (s32[64,1]{0,1:T(1,128)S(1)}, s32[64,1]{0,1:T(1,128)}, u32[]{:S(2)}) copy-start(s32[64,1]{0,1:T(1,128)} %param.13) | copy-start | bytes 772
  5.3 26.2 %copy-start = (f32[2048,128]{1,0:T(8,128)S(1)}, f32[2048,128]{1,0:T(8,128)}, u32[]{:S(2)}) copy-start(f32[2048,128]{1,0:T(8,128)} %pack.1) | copy-start | bytes 3145732
  6.5 28.7 %copy-start.6 = (f32[48]{0:T(128)S(1)}, f32[48]{0:T(128)}, u32[]{:S(2)}) copy-start(f32[48]{0:T(128)} %param.18) | copy-start | bytes 580
  6.5 9.6 %collective-permute-start = (f32[1,4,16,8,128]{4,3,2,1,0:T(8,128)S(1)}, f32[1,4,16,8,128]{4,3,2,1,0:T(8,128)S(1)}, u32[]{:S(2)}, u32[]{:S(2)}) collective-permute-start(f32[1,4,16,8,128]{4,3,2,1,0:T(8,128)S(1)} %bitcast.53), channel_id=1, source_target_pairs={{0,32},{32,64},{64,96},{96,0},{1,33},{33,65},{65,97},{97,1},{2,34}... | collective-permute-start | bytes 786440 | tf_op jit(solution)/shard_map/ppermute | solution.py:388
  10.7 7.3 %collective-permute-start.1 = (f32[1,4,16,8,128]{4,3,2,1,0:T(8,128)S(1)}, f32[1,4,16,8,128]{4,3,2,1,0:T(8,128)S(1)}, u32[]{:S(2)}, u32[]{:S(2)}) collective-permute-start(f32[1,4,16,8,128]{4,3,2,1,0:T(8,128)S(1)} %bitcast.52), channel_id=1, source_target_pairs={{32,0},{64,32},{96,64},{0,96},{33,1},{65,33},{97,65},{1,97},{34,2}... | collective-permute-start | bytes 786440 | tf_op jit(solution)/shard_map/ppermute | solution.py:389
  19.1 11.8 %collective-permute-start.2 = (f32[6,1,16,8,128]{4,3,2,1,0:T(8,128)S(1)}, f32[6,1,16,8,128]{4,3,2,1,0:T(8,128)S(1)}, u32[]{:S(2)}, u32[]{:S(2)}) collective-permute-start(f32[6,1,16,8,128]{4,3,2,1,0:T(8,128)S(1)} %get-tuple-element.6), channel_id=1, source_target_pairs={{0,8},{8,16},{16,24},{24,0},{1,9},{9,17},{17,25},{25,1},{2,10},{10... | collective-permute-start | bytes 1179656 | tf_op jit(solution)/shard_map/ppermute | solution.py:388
  20.5 11.0 %collective-permute-start.3 = (f32[6,1,16,8,128]{4,3,2,1,0:T(8,128)S(1)}, f32[6,1,16,8,128]{4,3,2,1,0:T(8,128)S(1)}, u32[]{:S(2)}, u32[]{:S(2)}) collective-permute-start(f32[6,1,16,8,128]{4,3,2,1,0:T(8,128)S(1)} %get-tuple-element.7), channel_id=1, source_target_pairs={{8,0},{16,8},{24,16},{0,24},{9,1},{17,9},{25,17},{1,25},{10,2},{18... | collective-permute-start | bytes 1179656 | tf_op jit(solution)/shard_map/ppermute | solution.py:389
  31.5 7.2 %collective-permute-start.4 = (f32[6,6,1,8,128]{4,3,2,1,0:T(8,128)S(1)}, f32[6,6,1,8,128]{4,3,2,1,0:T(8,128)S(1)}, u32[]{:S(2)}, u32[]{:S(2)}) collective-permute-start(f32[6,6,1,8,128]{4,3,2,1,0:T(8,128)S(1)} %get-tuple-element.4), channel_id=1, source_target_pairs={{0,1},{1,2},{2,3},{3,4},{4,5},{5,6},{6,7},{7,0},{8,9},{9,10},{10,1... | collective-permute-start | bytes 442376 | tf_op jit(solution)/shard_map/ppermute | solution.py:388
  33.2 5.5 %collective-permute-start.5 = (f32[6,6,1,8,128]{4,3,2,1,0:T(8,128)S(1)}, f32[6,6,1,8,128]{4,3,2,1,0:T(8,128)S(1)}, u32[]{:S(2)}, u32[]{:S(2)}) collective-permute-start(f32[6,6,1,8,128]{4,3,2,1,0:T(8,128)S(1)} %get-tuple-element.5), channel_id=1, source_target_pairs={{1,0},{2,1},{3,2},{4,3},{5,4},{6,5},{7,6},{0,7},{9,8},{10,9},{11,1... | collective-permute-start | bytes 442376 | tf_op jit(solution)/shard_map/ppermute | solution.py:389
  40.4 133.9 %copy-start.3 = (f32[6,48]{1,0:T(8,128)S(1)}, f32[6,48]{1,0:T(8,128)}, u32[]{:S(2)}) copy-start(f32[6,48]{1,0:T(8,128)} %param.16) | copy-start | bytes 3460
  40.4 133.9 %copy-start.4 = (f32[48]{0:T(128)S(1)}, f32[48]{0:T(128)}, u32[]{:S(2)}) copy-start(f32[48]{0:T(128)} %param.17) | copy-start | bytes 580
  40.4 133.9 %copy-start.5 = (f32[3]{0:T(128)S(1)}, f32[3]{0:T(128)}, u32[]{:S(2)}) copy-start(f32[3]{0:T(128)} %constant.65) | copy-start | bytes 40
  150.9 22.2 %all-to-all-start = ((f32[7,128,2]{0,2,1:T(2,128)}), f32[7,128,2]{0,2,1:T(2,128)S(1)}, u32[]{:S(2)}, u32[]{:S(2)}) async-start(f32[7,128,2]{0,2,1:T(2,128)} %bitcast.15), calls=%async_computation | async-start | bytes 262144 | tf_op jit(solution)/shard_map/all_to_all | solution.py:419
  174.5 20.8 %copy-start.1 = (f32[6,48]{1,0:T(8,128)}, f32[6,48]{1,0:T(8,128)S(1)}, u32[]{:S(2)}) copy-start(f32[6,48]{1,0:T(8,128)S(1)} %pad_maximum_fusion.9) | copy-start | bytes 3460
  176.3 14.1 %all-to-all-start.1 = ((f32[6,128,2]{0,2,1:T(2,128)}), f32[6,128,2]{0,2,1:T(2,128)S(1)}, u32[]{:S(2)}, u32[]{:S(2)}) async-start(f32[6,128,2]{0,2,1:T(2,128)} %broadcast_select_fusion), calls=%async_computation.1 | async-start | bytes 262144 | tf_op jit(solution)/shard_map/all_to_all | solution.py:428

commit v3 on v2

--- a/solution.py
+++ b/solution.py
@@ -8,6 +8,7 @@
 from jax.sharding import PartitionSpec as P
 
 CAP = 2
+OWN = 48
 QUICK = 6
 GROUP = 8
 REACH = 0.14001
@@ -29,13 +30,146 @@
     ]
 
 
-def pack_kernel(state, frag, table, out):
-    keys = jnp.broadcast_to(table[...], (8, 128))
+MESH = pl.DeviceIdType.MESH
+HBM = pl.BlockSpec(memory_space=pl.ANY)
+
+
+def place_of(shift):
+    return tuple(
+        lax.rem(lax.axis_index(axis) + step + lax.axis_size(axis), lax.axis_size(axis))
+        for axis, step in zip(("gx", "gy", "gz"), shift)
+    )
+
+
+def meet(others):
+    barrier = pltpu.get_barrier_semaphore()
+    for other in others:
+        pl.semaphore_signal(barrier, inc=1, device_id=other, device_id_type=MESH)
+    return lambda: pl.semaphore_wait(barrier, len(others))
+
+
+def halo_kernel(state, frag, info, out, own, send, recv, near):
+    sizes = out.shape[0] - 2, out.shape[1] - 2, out.shape[2] - 2
+    shifts = [(o // 9 - 1, o // 3 % 3 - 1, o % 3 - 1) for o in range(27) if o != 13]
+    shifts.sort(key=lambda s: sum(map(abs, s)))
+    arrive = meet([place_of(s) for s in shifts])
+    keys = info[0:1, :] * OWN + info[1:2, :]
+    keys = jnp.broadcast_to(keys.astype(jnp.float32), (8, 128))
     for g in range(frag.shape[0] // 8):
         rows = pl.ds(8 * g, 8)
         for k in range(7):
-            out[pl.ds(64 * g + k, 8, stride=8), :] = state[k, rows, :]
-        out[pl.ds(64 * g + 7, 8, stride=8), :] = lane_take(keys, frag[rows, :])
+            own[pl.ds(64 * g + k, 8, stride=8), :] = state[k, rows, :]
+        own[pl.ds(64 * g + 7, 8, stride=8), :] = lane_take(keys, frag[rows, :])
+    arrive()
+    cells = own.reshape(sizes + (8, 128))
+    copies = []
+    for n, shift in enumerate(shifts):
+        source = [pl.ds(0, size) if s == 0 else pl.ds(size - 1 if s > 0 else 0, 1) for s, size in zip(shift, sizes)]
+        target = [pl.ds(1, size) if s == 0 else pl.ds(0 if s > 0 else size + 1, 1) for s, size in zip(shift, sizes)]
+        copies.append(
+            pltpu.make_async_remote_copy(
+                src_ref=cells.at[tuple(source)],
+                dst_ref=out.at[tuple(target)],
+                send_sem=send.at[n],
+                recv_sem=recv.at[n],
+                device_id=place_of(shift),
+                device_id_type=MESH,
+            )
+        )
+        copies[-1].start()
+    inner = pltpu.make_async_copy(cells, out.at[tuple(pl.ds(1, size) for size in sizes)], near)
+    inner.start()
+    for copy in copies:
+        copy.wait()
+    inner.wait()
+
+
+def exchange_kernel(
+    info, sums, motion, mass, moment, table, clump_next,
+    outbox, got_z, got_y, inbox, reply, back_x, back_y, answer, send, recv, near,
+):
+    axes = ("gz", "gy", "gx")
+    me = {axis: lax.axis_index(axis) for axis in axes}
+    size = {axis: lax.axis_size(axis) for axis in axes}
+    peers = {
+        axis: [lax.rem(me[axis] + d, size[axis]) for d in range(1, size[axis])] for axis in axes
+    }
+
+    def device(axis, index):
+        return tuple(index if a == axis else me[a] for a in ("gx", "gy", "gz"))
+
+    arrive = meet([device(axis, p) for axis in axes for p in peers[axis]])
+
+    def stage(number, axis, source, target):
+        copies = [pltpu.make_async_copy(source(me[axis]), target(me[axis]), near.at[number])]
+        copies[0].start()
+        for n, peer in enumerate(peers[axis]):
+            copies.append(
+                pltpu.make_async_remote_copy(
+                    src_ref=source(peer),
+                    dst_ref=target(me[axis]),
+                    send_sem=send.at[number, n],
+                    recv_sem=recv.at[number, n],
+                    device_id=device(axis, peer),
+                    device_id_type=MESH,
+                )
+            )
+            copies[-1].start()
+        for copy in copies:
+            copy.wait()
+
+    exact = dict(precision=lax.Precision.HIGHEST, preferred_element_type=jnp.float32)
+    owner = info[0:1, :]
+    place = (owner & 7) * 16 + ((owner >> 3) & 3) * 4 + (owner >> 5)
+    place = jnp.where(owner >= 0, place, -1)
+    row = lax.broadcasted_iota(jnp.int32, (128, 128), 0)
+    col = lax.broadcasted_iota(jnp.int32, (128, 128), 1)
+    hit = (row == place).astype(jnp.float32)
+    earlier = jnp.dot(
+        hit.astype(jnp.bfloat16), (row < col).astype(jnp.float32).astype(jnp.bfloat16),
+        preferred_element_type=jnp.float32,
+    )
+    slots = [jnp.where(earlier == float(e), hit, 0.0) for e in range(CAP)]
+    across = (((1,), (1,)), ((), ()))
+    filler = jnp.zeros((112, 128), jnp.float32)
+    empty = jnp.zeros((8, 128), jnp.float32)
+    sub = lax.broadcasted_iota(jnp.int32, (8, 128), 0)
+    label = (info[1:2, :] + 1).astype(jnp.float32)
+    payload = jnp.where(sub == 6, label, jnp.where(sub == 7, 0.0, sums[...]))
+    outbox[...] = (
+        lax.dot_general(slots[0], jnp.concatenate([payload, empty, filler], axis=0), across, **exact)
+        + lax.dot_general(slots[1], jnp.concatenate([empty, payload, filler], axis=0), across, **exact)
+    ).reshape(outbox.shape)
+    arrive()
+    stage(0, "gz", lambda p: outbox.at[p], lambda p: got_z.at[:, p])
+    by_y = got_z.reshape(4, 4, 8, 128)
+    stage(1, "gy", lambda p: by_y.at[p], lambda p: got_y.at[:, p])
+    stage(2, "gx", lambda p: got_y.at[p], lambda p: inbox.at[p])
+
+    flat = inbox[...].reshape(128, 128)
+    turned = flat.T
+    names = lax.broadcasted_iota(jnp.int32, (128, motion.shape[1]), 1).astype(jnp.float32) + 1.0
+    which = [(jnp.broadcast_to(flat[:, 8 * e + 6 : 8 * e + 7], names.shape) == names).astype(jnp.float32) for e in range(CAP)]
+    total = jnp.dot(turned[0:8], which[0], **exact) + jnp.dot(turned[8:16], which[1], **exact)
+    lower = lax.broadcasted_iota(jnp.int32, (3, motion.shape[1]), 0)
+    pull = jnp.where(lower == 2, gravity, 0.0)
+    velocity = motion[0:3, :] + time_step * (total[0:3] * mass[...] - pull)
+    spin = motion[3:6, :] + time_step * total[3:6] * moment[...]
+    clump_next[0:3, :] = velocity
+    clump_next[3:6, :] = spin
+    moved = jnp.concatenate([velocity, spin, jnp.zeros((2, motion.shape[1]), jnp.float32)], axis=0)
+    blank = jnp.zeros((8, motion.shape[1]), jnp.float32)
+    rest = jnp.zeros((112, motion.shape[1]), jnp.float32)
+    reply[...] = (
+        lax.dot_general(which[0], jnp.concatenate([moved, blank, rest], axis=0), across, **exact)
+        + lax.dot_general(which[1], jnp.concatenate([blank, moved, rest], axis=0), across, **exact)
+    ).reshape(reply.shape)
+    stage(3, "gx", lambda p: reply.at[p], lambda p: back_x.at[p])
+    stage(4, "gy", lambda p: back_x.at[:, p], lambda p: back_y.at[p])
+    by_z = back_y.reshape(16, 8, 128)
+    stage(5, "gz", lambda p: by_z.at[:, p], lambda p: answer.at[p])
+    turned = answer[...].reshape(128, 128).T
+    table[...] = jnp.dot(turned[0:8], slots[0], **exact) + jnp.dot(turned[8:16], slots[1], **exact)
 
 
 def tiles_kernel(
@@ -261,7 +395,7 @@
         half(2 * p, wide_a, wide_b)
         half(2 * p + 1, wide_b, wide_a)
 
-    ids = lax.broadcasted_iota(jnp.int32, (64, 128), 0)
+    ids = lax.broadcasted_iota(jnp.int32, (128, 128), 0)
 
     def gather(g, total):
         rows = pl.ds(pl.multiple_of(g * 8, 8), 8)
@@ -285,7 +419,7 @@
         ).astype(jnp.bfloat16)
         return total + lax.dot_general(split, which, (((1,), (1,)), ((), ())), preferred_element_type=jnp.float32)
 
-    total = lax.fori_loop(0, owned // 8, gather, jnp.zeros((24, 64), jnp.float32))
+    total = lax.fori_loop(0, owned // 8, gather, jnp.zeros((24, 128), jnp.float32))
     out[...] = total[0:8] + total[8:16] + total[16:24]
 
 
@@ -308,21 +442,49 @@
             out[3 + k, rows, :] = velocity[k] + swing[k]
 
 
-def pack(state, frag, table):
-    n = frag.shape[0]
-    part = n // 4
+def halo(state, frag, info, cells):
     return pl.pallas_call(
-        pack_kernel,
-        grid=(4,),
-        in_specs=[
-            pl.BlockSpec((7, part, 128), lambda i: (0, i, 0)),
-            pl.BlockSpec((part, 128), lambda i: (i, 0)),
-            pl.BlockSpec((1, 128), lambda i: (0, 0)),
+        halo_kernel,
+        in_specs=[VMEM, VMEM, VMEM],
+        out_specs=HBM,
+        out_shape=jax.ShapeDtypeStruct(tuple(c + 2 for c in cells) + (8, 128), jnp.float32),
+        scratch_shapes=[
+            pltpu.VMEM((8 * frag.shape[0], 128), jnp.float32),
+            pltpu.SemaphoreType.DMA((26,)),
+            pltpu.SemaphoreType.DMA((26,)),
+            pltpu.SemaphoreType.DMA,
         ],
-        out_specs=pl.BlockSpec((8 * part, 128), lambda i: (i, 0)),
-        out_shape=jax.ShapeDtypeStruct((8 * n, 128), jnp.float32),
-        name="pack",
-    )(state, frag, table)
+        compiler_params=pltpu.CompilerParams(collective_id=0, has_side_effects=True),
+        name="halo",
+    )(state, frag, info)
+
+
+def exchange(info, sums, motion, mass, moment):
+    block = lambda *shape: pltpu.VMEM(shape + (128,), jnp.float32)
+    return pl.pallas_call(
+        exchange_kernel,
+        in_specs=[VMEM] * 5,
+        out_specs=(VMEM, VMEM),
+        out_shape=(
+            jax.ShapeDtypeStruct((8, 128), jnp.float32),
+            jax.ShapeDtypeStruct(motion.shape, jnp.float32),
+        ),
+        scratch_shapes=[
+            block(8, 16),
+            block(16, 8),
+            block(4, 4, 8),
+            block(4, 4, 8),
+            block(4, 4, 8),
+            block(4, 4, 8),
+            block(4, 4, 8),
+            block(8, 16),
+            pltpu.SemaphoreType.DMA((6, 7)),
+            pltpu.SemaphoreType.DMA((6, 7)),
+            pltpu.SemaphoreType.DMA((6,)),
+        ],
+        compiler_params=pltpu.CompilerParams(collective_id=1, has_side_effects=True),
+        name="exchange",
+    )(info, sums, motion, mass, moment)
 
 
 def forces(codes, cells, arms, frag):
@@ -332,7 +494,7 @@
         tiles_kernel,
         in_specs=[VMEM, VMEM, VMEM, VMEM],
         out_specs=VMEM,
-        out_shape=jax.ShapeDtypeStruct((8, 64), jnp.float32),
+        out_shape=jax.ShapeDtypeStruct((8, 128), jnp.float32),
         scratch_shapes=[
             pltpu.VMEM((cells.shape[0] // 8, 128), jnp.int32),
             pltpu.VMEM((lines * 128, 128), jnp.int32),
@@ -378,58 +540,18 @@
     )(state, arms, frag, table)
 
 
-def with_halo(x, sides):
-    for axis, dim in sides:
-        devices, length = (lax.axis_size(axis), x.shape[dim])
-        up = [(i, (i + 1) % devices) for i in range(devices)]
-        down = [(j, i) for i, j in up]
-        last = lax.slice_in_dim(x, length - 1, length, axis=dim)
-        initial = lax.slice_in_dim(x, 0, 1, axis=dim)
-        before = lax.ppermute(last, axis, up)
-        after = lax.ppermute(initial, axis, down)
-        x = jnp.concatenate([before, x, after], axis=dim)
-    return x
-
-
-def advance(motion, sums, inv_mass, inv_moment):
-    pull = jnp.array([0.0, 0.0, gravity], jnp.float32)[:, None]
-    velocity = motion[0:3] + time_step * (sums[0:3] * inv_mass[None, :] - pull)
-    spin = motion[3:6] + time_step * sums[3:6] * inv_moment[None, :]
-    return jnp.concatenate([velocity, spin], axis=0)
-
-
 def local(state, arms, sphere_frag, frag_owner, frag_clump, tiles, clump_motion, inv_mass, inv_moment):
-    cx, cy, cz, slots = state.shape[1:]
-    count = cx * cy * cz
-    owned = inv_mass.shape[0]
+    cells = state.shape[1:4]
+    slots = state.shape[4]
+    count = cells[0] * cells[1] * cells[2]
     held = frag_clump.shape[0]
-    bricks = lax.axis_size("gx") * lax.axis_size("gy") * lax.axis_size("gz")
-    owner = frag_owner[:, 0]
     frag = sphere_frag.reshape(count, slots)
-    key = (owner * owned + frag_clump).astype(jnp.float32)
-    own_cells = pack(state.reshape(7, count, slots), frag, jnp.pad(key, (0, 128 - held))[None])
-    padded = with_halo(own_cells.reshape(cx, cy, cz, 8, slots), (("gx", 0), ("gy", 1), ("gz", 2)))
-    frag_sums = forces(tiles[0], padded.reshape(-1, slots), arms.reshape(3, count, slots), frag)[0:6]
-
-    hits = (owner[:, None] == jnp.arange(bricks, dtype=jnp.int32)[None, :]).astype(jnp.int32)
-    rank = jnp.sum((jnp.cumsum(hits, axis=0) - hits) * hits, axis=1)
-    slot_index = owner * CAP + rank
-    payload = jnp.concatenate([frag_sums, (frag_clump + 1).astype(jnp.float32)[None]], axis=0)
-    outbox = jnp.zeros((7, bricks * CAP), jnp.float32).at[:, slot_index].set(payload)
-    inbox = lax.all_to_all(outbox, ("gx", "gy", "gz"), split_axis=1, concat_axis=1, tiled=True)
-    labels = (jnp.arange(owned, dtype=jnp.int32) + 1).astype(jnp.float32)
-    which = (inbox[6][:, None] == labels[None, :]).astype(jnp.float32)
-    clump_sums = jnp.dot(
-        inbox[0:6], which, precision=lax.Precision.HIGHEST, preferred_element_type=jnp.float32
-    )
-    clump_next = advance(clump_motion, clump_sums, inv_mass, inv_moment)
-    column = jnp.clip(inbox[6].astype(jnp.int32) - 1, 0, owned - 1)
-    reply = jnp.take(clump_next, column, axis=1)
-    answer = lax.all_to_all(reply, ("gx", "gy", "gz"), split_axis=1, concat_axis=1, tiled=True)
-    frag_motion = jnp.take(answer, slot_index, axis=1)
-    table = jnp.pad(frag_motion, ((0, 2), (0, 128 - held)))
+    info = jnp.pad(jnp.stack([frag_owner[:, 0], frag_clump]), ((0, 0), (0, slots - held)), constant_values=-1)
+    padded = halo(state.reshape(7, count, slots), frag, info, cells)
+    sums = forces(tiles[0], padded.reshape(-1, slots), arms.reshape(3, count, slots), frag)
+    table, clump_next = exchange(info, sums, clump_motion, inv_mass[None], inv_moment[None])
     sphere_next = move(state.reshape(7, count, slots), arms.reshape(3, count, slots), frag, table)
-    return sphere_next.reshape(6, cx, cy, cz, slots), clump_next
+    return sphere_next.reshape((6,) + cells + (slots,)), clump_next
 
 
 def solution(mesh):

time: 195 us -> 171 us (0.88)
  Pallas kernels: 115 us -> 166 us
  waiting for transfers between devices: 39.9 us -> 0 us
  starting transfers between devices: 27.2 us -> 0 us
  other arithmetic: 5.55 us -> 0.68 us
  local copies, waits for them, and re-layouts: 6.21 us -> 1.83 us
    pallas_call x1 -> x2, Pallas kernels: 3.51 us -> 53.7 us  [the longest x1 28.7 us: exchange(): pl.pallas_call(exchange_kernel, in_specs=[VMEM] * 5, out_specs=(VMEM, VME...]
    ppermute x6 -> x0, waiting for transfers between devices: 20 us -> none  [the longest x3 17.5 us: with_halo(): before = lax.ppermute(last, axis, up)]
    all_to_all x2 -> x0, waiting for transfers between devices: 19.9 us -> none  [the longest x1 9.96 us: local(): lax.all_to_all(outbox, ('gx', 'gy', 'gz'), split_axis=1, concat_axis=1, t...]
    all_to_all x2 -> x0, starting transfers between devices: 16.4 us -> none  [the longest x1 12.3 us: local(): lax.all_to_all(outbox, ('gx', 'gy', 'gz'), split_axis=1, concat_axis=1, t...]
    ppermute x6 -> x0, starting transfers between devices: 10.8 us -> none  [the longest x3 7.26 us: with_halo(): before = lax.ppermute(last, axis, up)]
    concatenate x3 -> x0, other arithmetic: 2.42 us -> none  [the longest x1 1.71 us: with_halo(): x = jnp.concatenate([before, x, after], axis=dim)]
  transfers between devices with their start and end apart: 8 -> 0, of which waited for: 7 -> 0; matrix products, arithmetic and copies ran while one was open for 0% -> 0% of each run, Pallas kernels for 0% -> 0%
where the time goes in v3:
time: 171 us; the launch traced here: 170 us
  Pallas kernels  166 us (97%)
  local copies, waits for them, and re-layouts  1.83 us (1%)
    pallas_call x1, Pallas kernels, forces(): pl.pallas_call(tiles_kernel, in_specs=[VMEM, VMEM, VMEM, VMEM], out_specs...  109 us
    pallas_call x1, Pallas kernels, exchange(): pl.pallas_call(exchange_kernel, in_specs=[VMEM] * 5, out_specs=(VMEM, VME...  28.7 us
    pallas_call x1, Pallas kernels, halo(): pl.pallas_call(halo_kernel, in_specs=[VMEM, VMEM, VMEM], out_specs=HBM, o...  25 us
    pallas_call x1, Pallas kernels, move(): pl.pallas_call(move_kernel, grid=(4,), in_specs=[pl.BlockSpec((3, part, 1...  3.62 us

profile of v3, /device:TPU:1, one launch (start us, length us, event | category | flops | bytes accessed | tf_op | source)
XLA Modules:
  0.0 169.5 jit_solution(13271722497126662085)
XLA Ops:
  0.6 0.7 pad_add_fusion
  1.3 0.6 pad.4.info
  1.9 25.0 %halo.1 = f32[6,6,18,8,128]{4,3,2,1,0:T(8,128)} custom-call(f32[7,256,128]{2,1,0:T(8,128)} %bitcast.11, s32[256,128]{1,0:T(8,128)} %bitcast.15, s32[2,128]{1,0:T(2,128)} %pad.4.info), custom_call_target="tpu_custom_call" | custom-call | tf_op jit(solution)/shard_map/halo/pallas_call | solution.py:446
  26.9 109.0 %forces.1.sums = f32[8,128]{1,0:T(8,128)} custom-call(s32[16,128]{1,0:T(8,128)} %bitcast.19, f32[5184,128]{1,0:T(8,128)} %bitcast.10, f32[3,256,128]{2,1,0:T(8,128)} %bitcast.13, s32[256,128]{1,0:T(8,128)} %bitcast.16), custom_call_target="tpu_custom_call" | custom-call | tf_op jit(solution)/shard_map/forces/pallas_call | solution.py:493
  135.9 28.7 %exchange.1 = (f32[8,128]{1,0:T(8,128)}, f32[6,48]{1,0:T(8,128)}) custom-call(s32[2,128]{1,0:T(2,128)} %pad.4.info, f32[8,128]{1,0:T(8,128)} %forces.1.sums, f32[6,48]{1,0:T(8,128)} %motion.1, f32[1,48]{1,0:T(1,128)} %bitcast.20, f32[1,48]{1,0:T(1,128)} %bitcast.21), custom_call_target="tpu_custom_call" | custom-call | tf_op jit(solution)/shard_map/exchange/pallas_call | solution.py:464
  164.6 3.6 %move.1 = f32[6,256,128]{2,1,0:T(8,128)} custom-call(f32[7,256,128]{2,1,0:T(8,128)} %bitcast.12, f32[3,256,128]{2,1,0:T(8,128)} %bitcast.14, s32[256,128]{1,0:T(8,128)} %bitcast.17, f32[8,128]{1,0:T(8,128)} %get-tuple-element.4.table), custom_call_target="tpu_custom_call" | custom-call | tf_op jit(solution)/shard_map/move/pallas_call | solution.py:528
  168.2 1.3 copy.12

commit v4 on v3

--- a/solution.py
+++ b/solution.py
@@ -9,7 +9,7 @@
 
 CAP = 2
 OWN = 48
-QUICK = 6
+QUICK = 8
 GROUP = 8
 REACH = 0.14001
 time_step = 0.01
@@ -48,11 +48,15 @@
     return lambda: pl.semaphore_wait(barrier, len(others))
 
 
-def halo_kernel(state, frag, info, out, own, send, recv, near):
+def halo_kernel(state, frag, owner, clump, out, info, own, send, recv, near):
     sizes = out.shape[0] - 2, out.shape[1] - 2, out.shape[2] - 2
     shifts = [(o // 9 - 1, o // 3 % 3 - 1, o % 3 - 1) for o in range(27) if o != 13]
     shifts.sort(key=lambda s: sum(map(abs, s)))
     arrive = meet([place_of(s) for s in shifts])
+    held = owner.shape[1]
+    info[...] = jnp.full(info.shape, -1, jnp.int32)
+    info[0:1, 0:held] = owner[...]
+    info[1:2, 0:held] = clump[...]
     keys = info[0:1, :] * OWN + info[1:2, :]
     keys = jnp.broadcast_to(keys.astype(jnp.float32), (8, 128))
     for g in range(frag.shape[0] // 8):
@@ -173,7 +177,7 @@
 
 
 def tiles_kernel(
-    codes, cells, arms, frag, out, cand, mask, counts, where_v, where_s, place_v, place_s, lens_v, lens_s, items,
+    codes, cells, arms, frag, out, cand, mask, counts, where_v, where_s, place_v, place_s, own_v, wide_v, lens_v, lens_s, items,
     carry, lists, shifts, wide_a, wide_b, push_x, push_y, push_z, loads, sems,
 ):
     pushes = (push_x, push_y, push_z)
@@ -195,13 +199,13 @@
     step_z = left - 3 * (step_y + 1) - 1
     cell_of = ((own_of >> 6) + 1 + step_x) * (ny * nz) + (((own_of >> 4) & 3) + 1 + step_y) * nz
     cell_of = cell_of + (own_of & 15) + 1 + step_z
-    where_v[...] = cell_of * 8 + (way << 16)
-    place_v[...] = own_of
+    for k, value in enumerate((cell_of, cell_of * 8, way, way * 8)):
+        where_v[k * lines : (k + 1) * lines, :] = value
+    own_v[...] = own_of
     first_copy = pltpu.make_async_copy(where_v, where_s, sems.at[0])
     first_copy.start()
 
-    @pl.loop(0, pad // 8)
-    def _(g):
+    def reach_bits(g):
         base = pl.multiple_of(g * 64, 64)
         pos = [cells[pl.ds(base + k, 8, stride=8), :] for k in range(3)]
         reach = cells[pl.ds(base + 6, 8, stride=8), :] + REACH
@@ -217,6 +221,11 @@
             bits = bits | jnp.where(sum(terms[1:], terms[0]) <= reach, 1 << o, 0)
         cand[pl.ds(pl.multiple_of(g * 8, 8), 8), :] = bits
 
+    @pl.loop(0, pad // 24)
+    def _(g):
+        for u in range(3):
+            reach_bits(3 * g + u)
+
     @pl.loop(0, 27)
     def _(o):
         step_x = ((o * 57) >> 9) - 1
@@ -234,12 +243,11 @@
 
     first_copy.wait()
 
-    @pl.loop(0, tiles // 16)
+    @pl.loop(0, lines)
     def _(b):
-        line, at = b >> 3, (b & 7) * 16
-        for u in range(16):
-            word = where_s[line, at + u]
-            mask[pl.ds(b * 16 + u, 1), :] = (cand[pl.ds((word & 0xFFFF) >> 3, 1), :] >> (word >> 16)) & 1
+        for u in range(128):
+            row = cand[pl.ds(where_s[b, u], 1), :]
+            mask[pl.ds(b * 128 + u, 1), :] = (row >> where_s[2 * lines + b, u]) & 1
 
     row = lax.broadcasted_iota(jnp.int32, (128, 128), 0)
     col = lax.broadcasted_iota(jnp.int32, (128, 128), 1)
@@ -267,18 +275,36 @@
 
     @pl.loop(0, lines)
     def _(b):
-        mine = place_v[pl.ds(b, 1), :]
+        mine = own_v[pl.ds(b, 1), :]
         hot = cell_id == mine
         amount = jnp.where(hot, counts[pl.ds(b, 1), :], 0.0)
         summed = jnp.dot(amount.astype(jnp.bfloat16), both, preferred_element_type=jnp.float32)
         so_far = carry[...]
         at = jnp.sum(jnp.where(hot, summed[:, 0:128] + so_far, 0.0), axis=0, keepdims=True)
         carry[...] = so_far + summed[:, 128:256]
-        place_v[pl.ds(b, 1), :] = mine * (depth * 128) + at.astype(jnp.int32)
-
-    length = carry[...].T[0:8, :]
-    most = jnp.max(length, axis=1, keepdims=True)
-    lens_v[...] = jnp.where(lax.broadcasted_iota(jnp.int32, (8, owned), 0) == 0, length, most).astype(jnp.int32)
+        spot = mine * (depth * 128) + at.astype(jnp.int32)
+        place_v[pl.ds(b, 1), :] = (spot >> 7) << 3
+        place_v[pl.ds(lines + b, 1), :] = spot & 127
+
+    length = carry[...].astype(jnp.int32)
+    cell_lane = lax.broadcasted_iota(jnp.int32, (owned, 128), 1)
+    words = (
+        cell_id * (depth * 8) + ((length >> 7) << 3),
+        length & 127,
+        jnp.minimum((length + 63) >> 6, QUICK),
+        (cell_id << 16) + cell_id * (2 * depth),
+        length,
+        jnp.broadcast_to(jnp.max(length, axis=0, keepdims=True), (owned, 128)),
+    )
+    packed = words[0]
+    for k, word in enumerate(words[1:]):
+        packed = jnp.where((cell_lane & 15) == k + 1, word, packed)
+    wide_v[...] = packed
+    eight = lax.broadcasted_iota(jnp.int32, (owned // 8, 128), 1) >> 4
+    folded = wide_v[pl.ds(0, owned // 8, stride=8), :]
+    for u in range(1, 8):
+        folded = jnp.where(eight == u, wide_v[pl.ds(u, owned // 8, stride=8), :], folded)
+    lens_v[...] = folded
     copies = [
         pltpu.make_async_copy(place_v, place_s, sems.at[1]),
         pltpu.make_async_copy(lens_v, lens_s, sems.at[2]),
@@ -288,49 +314,43 @@
     for copy in copies:
         copy.wait()
 
-    def append(sorted_rows, spot):
-        turn = spot & 127
-        to = pl.multiple_of((spot >> 7) * 8, 8)
+    def append(sorted_rows, to, turn):
+        to = pl.multiple_of(to, 8)
         turned = pltpu.roll(sorted_rows, turn, axis=1)
         pltpu.store(lists.at[pl.ds(to, 8), :], turned, mask=lane >= turn)
         lists[pl.ds(to + 8, 8), :] = turned
 
-    @pl.loop(0, tiles // 16)
+    @pl.loop(0, lines)
     def _(b):
-        line, at = b >> 3, (b & 7) * 16
-        for u in range(16):
-            word = where_s[line, at + u]
-            values = cells[pl.ds(pl.multiple_of(word & 0xFFFF, 8), 8), :]
-            index = jnp.broadcast_to(mask[pl.ds(b * 16 + u, 1), :], (8, 128))
-            shift = shifts[pl.ds(pl.multiple_of((word >> 16) * 8, 8), 8), :]
-            append(lane_take(values, index) + shift, place_s[line, at + u])
+        for u in range(128):
+            values = cells[pl.ds(pl.multiple_of(where_s[lines + b, u], 8), 8), :]
+            index = jnp.broadcast_to(mask[pl.ds(b * 128 + u, 1), :], (8, 128))
+            shift = shifts[pl.ds(pl.multiple_of(where_s[3 * lines + b, u], 8), 8), :]
+            append(lane_take(values, index) + shift, place_s[b, u], place_s[lines + b, u])
 
     dummy = jnp.where(sub < 3, 1000.0, 0.1)
-
-    def item(c, k):
-        return (c << 16) | (c * (2 * depth) + k)
 
     def close(b, total):
         for u in range(8):
-            c = b * 8 + u
-            length = lens_s[0, c]
-            append(dummy, c * (depth * 128) + length)
+            append(dummy, lens_s[b, 16 * u], lens_s[b, 16 * u + 1])
+            first = lens_s[b, 16 * u + 3]
             for k in range(QUICK):
-                items[total + k] = item(c, k)
-            total = total + jnp.minimum((length + 63) >> 6, QUICK)
+                items[total + k] = first + k
+            total = total + lens_s[b, 16 * u + 2]
         return total
 
     number = lax.fori_loop(0, owned // 8, close, 0)
 
     def longer(c, total):
+        line, at = c >> 3, (c & 7) * 16
+
         def add(k, total):
-            items[total] = item(c, k)
+            items[total] = lens_s[line, at + 3] + k
             return total + 1
 
-        return lax.fori_loop(QUICK, (lens_s[0, c] + 63) >> 6, add, total)
-
-    longest = lens_s[1, 0]
-    number = lax.fori_loop(0, jnp.where(longest > 64 * QUICK, owned, 0), longer, number)
+        return lax.fori_loop(QUICK, (lens_s[line, at + 4] + 63) >> 6, add, total)
+
+    number = lax.fori_loop(0, jnp.where(lens_s[0, 5] > 64 * QUICK, owned, 0), longer, number)
     for k in range(3 * GROUP):
         items[number + k] = owned << 16
 
@@ -423,7 +443,8 @@
     out[...] = total[0:8] + total[8:16] + total[16:24]
 
 
-def move_kernel(state, arms, frag, table, out):
+def move_kernel(state, arms, frag, table, clump_next, out, clump_out):
+    clump_out[...] = clump_next[...]
     rows_of = [jnp.broadcast_to(table[k : k + 1, :], (8, 128)) for k in range(6)]
     for g in range(frag.shape[0] // 8):
         rows = pl.ds(8 * g, 8)
@@ -442,12 +463,15 @@
             out[3 + k, rows, :] = velocity[k] + swing[k]
 
 
-def halo(state, frag, info, cells):
+def halo(state, frag, owner, clump, cells):
     return pl.pallas_call(
         halo_kernel,
-        in_specs=[VMEM, VMEM, VMEM],
-        out_specs=HBM,
-        out_shape=jax.ShapeDtypeStruct(tuple(c + 2 for c in cells) + (8, 128), jnp.float32),
+        in_specs=[VMEM] * 4,
+        out_specs=(HBM, VMEM),
+        out_shape=(
+            jax.ShapeDtypeStruct(tuple(c + 2 for c in cells) + (8, 128), jnp.float32),
+            jax.ShapeDtypeStruct((2, 128), jnp.int32),
+        ),
         scratch_shapes=[
             pltpu.VMEM((8 * frag.shape[0], 128), jnp.float32),
             pltpu.SemaphoreType.DMA((26,)),
@@ -456,7 +480,7 @@
         ],
         compiler_params=pltpu.CompilerParams(collective_id=0, has_side_effects=True),
         name="halo",
-    )(state, frag, info)
+    )(state, frag, owner, clump)
 
 
 def exchange(info, sums, motion, mass, moment):
@@ -499,12 +523,14 @@
             pltpu.VMEM((cells.shape[0] // 8, 128), jnp.int32),
             pltpu.VMEM((lines * 128, 128), jnp.int32),
             pltpu.VMEM((lines, 128), jnp.float32),
+            pltpu.VMEM((4 * lines, 128), jnp.int32),
+            pltpu.SMEM((4 * lines, 128), jnp.int32),
+            pltpu.VMEM((2 * lines, 128), jnp.int32),
+            pltpu.SMEM((2 * lines, 128), jnp.int32),
             pltpu.VMEM((lines, 128), jnp.int32),
-            pltpu.SMEM((lines, 128), jnp.int32),
-            pltpu.VMEM((lines, 128), jnp.int32),
-            pltpu.SMEM((lines, 128), jnp.int32),
-            pltpu.VMEM((8, owned), jnp.int32),
-            pltpu.SMEM((8, owned), jnp.int32),
+            pltpu.VMEM((owned, 128), jnp.int32),
+            pltpu.VMEM((owned // 8, 128), jnp.int32),
+            pltpu.SMEM((owned // 8, 128), jnp.int32),
             pltpu.SMEM((owned * 54 + 32,), jnp.int32),
             pltpu.VMEM((owned, 128), jnp.float32),
             pltpu.VMEM((owned * depth * 8, 128), jnp.float32),
@@ -522,7 +548,7 @@
     )(codes.reshape(lines, 128), cells, arms, frag)
 
 
-def move(state, arms, frag, table):
+def move(state, arms, frag, table, clump_next):
     n = frag.shape[0]
     part = n // 4
     return pl.pallas_call(
@@ -533,11 +559,18 @@
             pl.BlockSpec((3, part, 128), lambda i: (0, i, 0)),
             pl.BlockSpec((part, 128), lambda i: (i, 0)),
             pl.BlockSpec((8, 128), lambda i: (0, 0)),
+            pl.BlockSpec(clump_next.shape, lambda i: (0, 0)),
         ],
-        out_specs=pl.BlockSpec((6, part, 128), lambda i: (0, i, 0)),
-        out_shape=jax.ShapeDtypeStruct((6, n, 128), jnp.float32),
+        out_specs=(
+            pl.BlockSpec((6, part, 128), lambda i: (0, i, 0)),
+            pl.BlockSpec(clump_next.shape, lambda i: (0, 0)),
+        ),
+        out_shape=(
+            jax.ShapeDtypeStruct((6, n, 128), jnp.float32),
+            jax.ShapeDtypeStruct(clump_next.shape, jnp.float32),
+        ),
         name="move",
-    )(state, arms, frag, table)
+    )(state, arms, frag, table, clump_next)
 
 
 def local(state, arms, sphere_frag, frag_owner, frag_clump, tiles, clump_motion, inv_mass, inv_moment):
@@ -546,11 +579,12 @@
     count = cells[0] * cells[1] * cells[2]
     held = frag_clump.shape[0]
     frag = sphere_frag.reshape(count, slots)
-    info = jnp.pad(jnp.stack([frag_owner[:, 0], frag_clump]), ((0, 0), (0, slots - held)), constant_values=-1)
-    padded = halo(state.reshape(7, count, slots), frag, info, cells)
+    padded, info = halo(state.reshape(7, count, slots), frag, frag_owner.reshape(1, held), frag_clump[None], cells)
     sums = forces(tiles[0], padded.reshape(-1, slots), arms.reshape(3, count, slots), frag)
     table, clump_next = exchange(info, sums, clump_motion, inv_mass[None], inv_moment[None])
-    sphere_next = move(state.reshape(7, count, slots), arms.reshape(3, count, slots), frag, table)
+    sphere_next, clump_next = move(
+        state.reshape(7, count, slots), arms.reshape(3, count, slots), frag, table, clump_next
+    )
     return sphere_next.reshape((6,) + cells + (slots,)), clump_next
 
 

time: 171 us -> 152 us (0.89)
  Pallas kernels: 166 us -> 150 us
  local copies, waits for them, and re-layouts: 1.83 us -> 0 us
    pallas_call x1, Pallas kernels: 109 us -> 91.3 us  [forces(): pl.pallas_call(tiles_kernel, in_specs=[VMEM, VMEM, VMEM, VMEM], out_specs...]
where the time goes in v4:
time: 152 us; the launch traced here: 151 us
  Pallas kernels  150 us (99%)
    pallas_call x1, Pallas kernels, forces(): pl.pallas_call(tiles_kernel, in_specs=[VMEM, VMEM, VMEM, VMEM], out_specs...  91.3 us
    pallas_call x1, Pallas kernels, exchange(): pl.pallas_call(exchange_kernel, in_specs=[VMEM] * 5, out_specs=(VMEM, VME...  29.6 us
    pallas_call x1, Pallas kernels, halo(): pl.pallas_call(halo_kernel, in_specs=[VMEM] * 4, out_specs=(HBM, VMEM), o...  25.7 us
    pallas_call x1, Pallas kernels, move(): pl.pallas_call(move_kernel, grid=(4,), in_specs=[pl.BlockSpec((3, part, 1...  3.63 us

profile of v4, /device:TPU:1, one launch (start us, length us, event | category | flops | bytes accessed | tf_op | source)
XLA Modules:
  0.0 150.9 jit_solution(10277429086414200849)
XLA Ops:
  0.6 25.7 %halo.1 = (f32[6,6,18,8,128]{4,3,2,1,0:T(8,128)}, s32[2,128]{1,0:T(2,128)}) custom-call(f32[7,256,128]{2,1,0:T(8,128)} %bitcast.10, s32[256,128]{1,0:T(8,128)} %bitcast.15, s32[1,64]{1,0:T(1,128)} %bitcast.19, s32[1,64]{1,0:T(1,128)} %bitcast.20), custom_call_target="tpu_custom_call" | custom-call | tf_op jit(solution)/shard_map/halo/pallas_call | solution.py:467
  26.4 91.3 %forces.1.sums = f32[8,128]{1,0:T(8,128)} custom-call(s32[16,128]{1,0:T(8,128)} %bitcast.18, f32[5184,128]{1,0:T(8,128)} %bitcast.12, f32[3,256,128]{2,1,0:T(8,128)} %bitcast.13, s32[256,128]{1,0:T(8,128)} %bitcast.16), custom_call_target="tpu_custom_call" | custom-call | tf_op jit(solution)/shard_map/forces/pallas_call | solution.py:517
  117.6 29.6 %exchange.1 = (f32[8,128]{1,0:T(8,128)}, f32[6,48]{1,0:T(8,128)}) custom-call(s32[2,128]{1,0:T(2,128)} %get-tuple-element.8.info, f32[8,128]{1,0:T(8,128)} %forces.1.sums, f32[6,48]{1,0:T(8,128)} %motion.1, f32[1,48]{1,0:T(1,128)} %bitcast.21, f32[1,48]{1,0:T(1,128)} %bitcast.22), custom_call_target="tpu_custom_call" | custom-call | tf_op jit(solution)/shard_map/exchange/pallas_call | solution.py:488
  147.3 3.6 %move.1 = (f32[6,256,128]{2,1,0:T(8,128)}, f32[6,48]{1,0:T(8,128)}) custom-call(f32[7,256,128]{2,1,0:T(8,128)} %bitcast.11, f32[3,256,128]{2,1,0:T(8,128)} %bitcast.14, s32[256,128]{1,0:T(8,128)} %bitcast.17, f32[8,128]{1,0:T(8,128)} %get-tuple-element.10.table, f32[6,48]{1,0:T(8,128)} %get-tuple-element.11.clump_next), custom_call_target="tpu_custom_call" | custom-call | tf_op jit(solution)/shard_map/move/pallas_call | solution.py:554
